TPU v7x, 128 devices: a whole 4x4x4 slice. The times are simulated.
128 devices in a mesh: row: 8 (over x, z_lo), col: 16 (over z_hi, y, core).
Axes of the slice: x: 4, y: 4, z: 4 (z_hi: 2, z_lo: 2; z = z_hi * 2 + z_lo), core: 2. Of those that a mesh axis runs over, the one named last changes fastest.
Arguments:
- a_cols: bfloat16 [16384, 8192], P('row', 'col'), may hold values from -6 to 6
- owners: int32 [1024], replicated, may hold values from 0 to 15
- column_slot: int32 [1024], replicated, may hold values from 0 to 511
- update_flag: int32 [1024], replicated, may hold values from 0 to 1
- rescale: float32 [1024], replicated, may hold values from 0.5 to 2
- inverses: bfloat16 [2, 512, 512], replicated, may hold values from -0.0078125 to 0.0078125
- trailing: float32 [16384, 16384], P('row', 'col'), may hold values from -0.15625 to 0.15625
Outputs:
- updated_slab: float32 [16384, 16384], P('row', 'col')
- panels: bfloat16 [16384, 1024], P('row')
All inputs are finite; a program needn't handle non-finite values.
Results may differ from a plain program's by a relative error of at most 0.013.
The roundings to bfloat16 on the way count: a program that leaves them out, or rounds other values in their place, can miss the bound.
Values may be sent and summed in bfloat16 or wider, within the bound.
No kernel may reach another device: no remote copies, remote signals or barrier semaphores. Data moves between devices by JAX's collectives and lax.ppermute only.
A program may use at most 128 MiB of HBM per device.

v0:
```python
import jax
import jax.numpy as jnp
from jax import lax
from jax.experimental import pallas as pl
from jax.experimental.pallas import tpu as pltpu
from jax.sharding import PartitionSpec as P


BF = jnp.bfloat16
F32 = jnp.float32


def move(value, route):
    pairs = []
    for x in range(4):
        for zl in range(2):
            for zh in range(2):
                for y in range(4):
                    for k in range(2):
                        x2, zl2, zh2, y2, k2 = route(x, zl, zh, y, k)
                        source = (x * 2 + zl) * 16 + zh * 8 + y * 2 + k
                        target = (x2 % 4 * 2 + zl2) * 16 + zh2 * 8 + y2 % 4 * 2 + k2
                        pairs.append((source, target))
    return lax.ppermute(value, ("row", "col"), pairs)


def other_core(x, zl, zh, y, k):
    return x, zl, zh, y, 1 - k


def other_zh(x, zl, zh, y, k):
    return x, zl, 1 - zh, y, k


def other_zl(x, zl, zh, y, k):
    return x, 1 - zl, zh, y, k


def along_y(step):
    return lambda x, zl, zh, y, k: (x, zl, zh, y + step, k)


def along_x(step):
    return lambda x, zl, zh, y, k: (x + step, zl, zh, y, k)


def flip_x(bit):
    return lambda x, zl, zh, y, k: (x ^ bit, zl, zh, y, k)


def flip_y(bit):
    return lambda x, zl, zh, y, k: (x, zl, zh, y ^ bit, k)


def to_strip(x, zl, zh, y, k):
    zh2 = x // 2
    return x + y, zh ^ zl ^ zh2, zh2, (x % 2) * 2 + zl, k


def rows(value, start, count):
    return lax.dynamic_slice_in_dim(value, start, count, 0)


def joined(mine, theirs, mine_second, axis):
    return jnp.where(
        mine_second == 1,
        jnp.concatenate([theirs, mine], axis),
        jnp.concatenate([mine, theirs], axis),
    )


def mm(a, b):
    return jnp.dot(a, b, preferred_element_type=F32)


def to_chip(step, dz):
    return lambda x, zl, zh, y, k: (x, zl, zh ^ dz, y + step, k)


def second_panel(cols, inverse, gram, sign):
    weighted = cols[:, :512] * sign[:, :512]
    coupled = (cols[:, 512:].astype(F32) - mm(weighted, gram[...])).astype(BF)
    return mm(coupled, inverse[...]).astype(BF)


SLAB = 512
SLABS = 2048 // SLAB


def tail_kernel(spot, *refs):
    pieces = refs[:17]
    inverses, sign, trailing, out, panels = refs[17:22]
    cols, strip, block, slab, gram_here, inverse_here = refs[22:28]
    piece_sem, fixed_sem, load_sem, save_sem, panel_sem = refs[28:]

    def fetch(i):
        if i >= 24:
            source, target, height = pieces[15 + i - 24], gram_here, 256
        else:
            group, half = i // 8, i % 8
            source = pieces[group * 5 + (half // 2 if half < 6 else half - 3)]
            if half < 6:
                source = source.at[pl.ds(half % 2 * 128, 128)]
            target, height = cols if group == 0 else block, 128
        at = pl.ds(pl.multiple_of(spot[i] * 128, 128), height)
        return pltpu.make_async_copy(source, target.at[at], piece_sem.at[i])

    def rows_of(i):
        return pl.ds(pl.multiple_of(i * SLAB, SLAB), SLAB)

    def load(i):
        return pltpu.make_async_copy(
            trailing.at[rows_of(i)], slab.at[rows_of(i)], load_sem.at[i]
        )

    def save(i):
        return pltpu.make_async_copy(slab.at[rows_of(i)], out.at[rows_of(i)], save_sem.at[i])

    def save_panel(i):
        return pltpu.make_async_copy(
            block.at[rows_of(i)], panels.at[rows_of(i)], panel_sem.at[i]
        )

    constants = pltpu.make_async_copy(inverses.at[1], inverse_here, fixed_sem)
    constants.start()
    early = (*range(8), 24, 25)
    for i in early:
        fetch(i).start()
    for i in range(8, 24):
        fetch(i).start()
    for i in range(SLABS):
        load(i).start()

    for i in early:
        fetch(i).wait()
    constants.wait()
    second = second_panel(cols, inverse_here, gram_here, sign[...])
    strip[:, :512] = cols[:, :512] * sign[:, :512]
    strip[:, 512:] = second * sign[:, 512:]
    for i in range(8, 24):
        fetch(i).wait()

    def step(i, carry):
        at = rows_of(i)
        block[at, 512:] = second_panel(block.at[at], inverse_here, gram_here, sign[...])
        save_panel(i).start()
        load(i).wait()
        slab[at, :] = slab[at, :] + lax.dot_general(
            block[at, :],
            strip[...],
            (((1,), (1,)), ((), ())),
            preferred_element_type=F32,
        )
        save(i).start()
        return carry

    lax.fori_loop(0, SLABS, step, 0)
    for i in range(SLABS):
        save_panel(i).wait()
        save(i).wait()


def tail(spot, pieces, inverses, sign, trailing):
    anywhere = pl.BlockSpec(memory_space=pl.ANY)
    return pl.pallas_call(
        tail_kernel,
        grid_spec=pltpu.PrefetchScalarGridSpec(
            num_scalar_prefetch=1,
            grid=(1,),
            in_specs=[anywhere] * 18
            + [pl.BlockSpec((1, 1024), lambda t, spot: (0, 0)), anywhere],
            out_specs=[anywhere] * 2,
            scratch_shapes=[
                pltpu.VMEM((1024, 1024), BF),
                pltpu.VMEM((1024, 1024), BF),
                pltpu.VMEM((2048, 1024), BF),
                pltpu.VMEM((2048, 1024), F32),
                pltpu.VMEM((512, 512), BF),
                pltpu.VMEM((512, 512), BF),
                pltpu.SemaphoreType.DMA((26,)),
                pltpu.SemaphoreType.DMA,
                pltpu.SemaphoreType.DMA((SLABS,)),
                pltpu.SemaphoreType.DMA((SLABS,)),
                pltpu.SemaphoreType.DMA((SLABS,)),
            ],
        ),
        out_shape=(
            jax.ShapeDtypeStruct((2048, 1024), F32),
            jax.ShapeDtypeStruct((2048, 1024), BF),
        ),
        compiler_params=pltpu.CompilerParams(vmem_limit_bytes=46 * 2**20),
        cost_estimate=pl.CostEstimate(
            flops=9_000_000_000, bytes_accessed=28 * 2**20, transcendentals=0
        ),
    )(spot, *pieces, inverses, sign, trailing)


def body(a_cols, owners, column_slot, update_flag, rescale, inverses, trailing):
    col = lax.axis_index("col")
    row = lax.axis_index("row")
    k, y, zh = col % 2, (col // 2) % 4, col // 8
    x, zl = row // 2, row % 2
    signed = (2 * update_flag - 1).astype(BF)

    keep = rows(a_cols, k * 1024, 1024)
    got = move(rows(a_cols, (1 - k) * 1024, 1024), other_core)
    chip = owners // 2
    stored = (owners % 2 ^ k) * 512 + column_slot
    square = (1024, 1024)
    before = lax.broadcasted_iota(jnp.int32, square, 0) < lax.broadcasted_iota(jnp.int32, square, 1)
    rank = jnp.sum((chip[:, None] == chip[None, :]) & before, axis=0, dtype=jnp.int32)

    def exchange(base):
        slot = lax.broadcasted_iota(jnp.int32, (1024, 512), 1)
        held = (chip == zh * 4 + y)[:, None] & ((rank - base)[:, None] == slot)
        origin = jnp.sum(jnp.where(held, stored[:, None] + 1, 0), axis=0) - 1
        pack = (lax.broadcasted_iota(jnp.int32, (1024, 512), 0) == origin[None, :]).astype(BF)
        packed = (mm(keep, pack[:512]) + mm(got, pack[512:])).astype(BF)
        slots = lax.broadcasted_iota(jnp.int32, (512, 1024), 0)
        total = None
        for dz in (0, 1):
            for step in (0, 1, 2, 3):
                piece = rows(packed, (y + step) % 4 * 256 + (zh ^ dz) * 128, 128)
                if dz or step:
                    piece = move(piece, to_chip(step, dz))
                there = chip == (zh ^ dz) * 4 + (y - step) % 4
                select = (slots == jnp.where(there, rank - base, -1)[None, :]).astype(BF)
                term = mm(piece, select)
                total = term if total is None else total + term
        return total

    picked = exchange(0)
    picked = lax.cond(
        jnp.max(rank) >= 512,
        lambda value: value + exchange(512),
        lambda value: value,
        picked,
    )
    cols = (picked * rescale[None, :]).astype(BF)
    cols = jnp.concatenate([mm(cols[:, :512], inverses[0]).astype(BF), cols[:, 512:]], axis=1)

    pair = jnp.concatenate([cols, move(cols, other_zh)], axis=0)

    first = zh * 2 + y // 2
    part = zl ^ (y % 2) ^ zh
    piece = move(cols, to_strip)
    strip = jnp.concatenate([piece, move(piece, other_zl)], axis=0)
    strips = [strip] + [move(strip, along_x(step)) for step in (1, 3)]
    across = move(piece, along_x(2))
    strips += [across, move(across, other_zl)]

    beyond = move(cols, along_y(2))
    near = [pair] + [move(pair, along_y(step)) for step in (1, 3)]
    near += [beyond, move(beyond, other_zh)]
    far = [move(value, other_core) for value in near]

    fp = pair[:, :512]
    right = lax.dynamic_slice_in_dim(pair, 512 + zh * 256, 256, 1)
    gram = lax.dot_general(fp, right, (((0,), (0,)), ((), ())), preferred_element_type=F32)
    gram = rows(gram, k * 256, 256) + move(rows(gram, (1 - k) * 256, 256), other_core)
    odd, high = y % 2, y // 2
    total = rows(gram, odd * 128, 128) + move(rows(gram, (1 - odd) * 128, 128), flip_y(1))
    total = rows(total, high * 64, 64) + move(rows(total, (1 - high) * 64, 64), flip_y(2))
    total = total + move(total, other_zl)
    one, two, three = [move(total, flip_x(bit)) for bit in (1, 2, 3)]
    total = (total + one) + (two + three)
    low = total.astype(BF)
    low = joined(low, move(low, other_zh), zh, 1)
    low = joined(low, move(low, flip_y(2)), high, 0)
    low = joined(low, move(low, flip_y(1)), odd, 0)
    grams = [low, move(low, other_core)]

    index = lax.iota(jnp.int32, 24)
    kind, index = index // 8, index % 8
    hop = jnp.where(index < 6, (index // 2 * (index // 2 + 1)) // 2, 2)
    lower = jnp.where(kind == 0, part, zh) ^ (index % 2)
    base = jnp.where(kind == 0, x - first, y)
    spot = (base - hop) % 4 * 2 + lower
    spot += jnp.where(kind == 0, 0, jnp.where(kind == 1, k, 1 - k)) * 8
    spot = jnp.concatenate([spot, jnp.stack([k, 1 - k]) * 2])
    return tail(spot, strips + near + far + grams, inverses, signed[None, :], trailing)


def solution(mesh):
    placed = (P("row", "col"), P(), P(), P(), P(), P(), P("row", "col"))
    return jax.shard_map(
        body,
        mesh=mesh,
        in_specs=placed,
        out_specs=(P("row", "col"), P("row", None)),
        check_vma=False,
    )
```

profile of v0, /device:TPU:8, one launch (start us, length us, event | category | flops | bytes accessed | tf_op | source)
XLA Modules:
  0.0 141.1 jit_solution(13863635443382473972)
XLA Ops:
  8.5 2.4 %collective-permute-start.9 = (bf16[128,512]{1,0:T(8,128)(2,1)S(1)}, bf16[128,512]{1,0:T(8,128)(2,1)S(1)}, u32[]{:S(2)}, u32[]{:S(2)}) collective-permute-start(bf16[128,512]{1,0:T(8,128)(2,1)S(1)} %get-tuple-element.53), channel_id=1, source_target_pairs={{0,4},{1,5},{2,6},{3,7},{4,0},{5,1},{6,2},{7,3},{8,12},{9,13},{10,... | collective-permute-start | bytes 393224 | tf_op jit(solution)/shard_map/ppermute | solution.py:24
  10.9 4.7 %collective-permute-start.14 = (bf16[128,512]{1,0:T(8,128)(2,1)S(1)}, bf16[128,512]{1,0:T(8,128)(2,1)S(1)}, u32[]{:S(2)}, u32[]{:S(2)}) collective-permute-start(bf16[128,512]{1,0:T(8,128)(2,1)S(1)} %get-tuple-element.54), channel_id=1, source_target_pairs={{0,14},{1,15},{2,8},{3,9},{4,10},{5,11},{6,12},{7,13},{8,6},{9,7},... | collective-permute-start | bytes 393224 | tf_op jit(solution)/shard_map/ppermute | solution.py:24
  15.6 4.9 %collective-permute-start.12 = (bf16[128,512]{1,0:T(8,128)(2,1)S(1)}, bf16[128,512]{1,0:T(8,128)(2,1)S(1)}, u32[]{:S(2)}, u32[]{:S(2)}) collective-permute-start(bf16[128,512]{1,0:T(8,128)(2,1)S(1)} %get-tuple-element.56), channel_id=1, source_target_pairs={{0,10},{1,11},{2,12},{3,13},{4,14},{5,15},{6,8},{7,9},{8,2},{9,3},... | collective-permute-start | bytes 393224 | tf_op jit(solution)/shard_map/ppermute | solution.py:24
  22.6 5.0 %collective-permute-done.8 = bf16[128,512]{1,0:T(8,128)(2,1)S(1)} collective-permute-done((bf16[128,512]{1,0:T(8,128)(2,1)S(1)}, bf16[128,512]{1,0:T(8,128)(2,1)S(1)}, u32[]{:S(2)}, u32[]{:S(2)}) %collective-permute-start.8) | collective-permute-done | bytes 131104 | tf_op jit(solution)/shard_map/ppermute | solution.py:24
  27.7 2.0 %collective-permute-start.10 = (bf16[128,512]{1,0:T(8,128)(2,1)S(1)}, bf16[128,512]{1,0:T(8,128)(2,1)S(1)}, u32[]{:S(2)}, u32[]{:S(2)}) collective-permute-start(bf16[128,512]{1,0:T(8,128)(2,1)S(1)} %get-tuple-element.58), channel_id=1, source_target_pairs={{0,6},{1,7},{2,0},{3,1},{4,2},{5,3},{6,4},{7,5},{8,14},{9,15},{10,... | collective-permute-start | bytes 393224 | tf_op jit(solution)/shard_map/ppermute | solution.py:24
  30.2 2.4 %collective-permute-done.10 = bf16[128,512]{1,0:T(8,128)(2,1)S(1)} collective-permute-done((bf16[128,512]{1,0:T(8,128)(2,1)S(1)}, bf16[128,512]{1,0:T(8,128)(2,1)S(1)}, u32[]{:S(2)}, u32[]{:S(2)}) %collective-permute-start.10) | collective-permute-done | bytes 131104 | tf_op jit(solution)/shard_map/ppermute | solution.py:24
  32.6 3.2 %collective-permute-start.11 = (bf16[128,512]{1,0:T(8,128)(2,1)S(1)}, bf16[128,512]{1,0:T(8,128)(2,1)S(1)}, u32[]{:S(2)}, u32[]{:S(2)}) collective-permute-start(bf16[128,512]{1,0:T(8,128)(2,1)S(1)} %get-tuple-element.57), channel_id=1, source_target_pairs={{0,8},{1,9},{2,10},{3,11},{4,12},{5,13},{6,14},{7,15},{8,0},{9,1},... | collective-permute-start | bytes 393224 | tf_op jit(solution)/shard_map/ppermute | solution.py:24
  36.3 2.8 %collective-permute-done.11 = bf16[128,512]{1,0:T(8,128)(2,1)S(1)} collective-permute-done((bf16[128,512]{1,0:T(8,128)(2,1)S(1)}, bf16[128,512]{1,0:T(8,128)(2,1)S(1)}, u32[]{:S(2)}, u32[]{:S(2)}) %collective-permute-start.11) | collective-permute-done | bytes 131104 | tf_op jit(solution)/shard_map/ppermute | solution.py:24
  43.4 3.2 %collective-permute-start.21 = (bf16[128,1024]{1,0:T(8,128)(2,1)S(1)}, bf16[128,1024]{1,0:T(8,128)(2,1)S(1)}, u32[]{:S(2)}, u32[]{:S(2)}) collective-permute-start(bf16[128,1024]{1,0:T(8,128)(2,1)S(1)} %pad_maximum_fusion.1), channel_id=1, source_target_pairs={{0,8},{1,9},{2,10},{3,11},{4,12},{5,13},{6,14},{7,15},{8,0},{9,1},... | collective-permute-start | bytes 786440 | tf_op jit(solution)/shard_map/ppermute | solution.py:24
  46.7 4.7 %collective-permute-done.21 = bf16[128,1024]{1,0:T(8,128)(2,1)S(1)} collective-permute-done((bf16[128,1024]{1,0:T(8,128)(2,1)S(1)}, bf16[128,1024]{1,0:T(8,128)(2,1)S(1)}, u32[]{:S(2)}, u32[]{:S(2)}) %collective-permute-start.21) | collective-permute-done | bytes 262176 | tf_op jit(solution)/shard_map/ppermute | solution.py:24
  53.4 2.1 %collective-permute-start.32 = (f32[128,256]{1,0:T(8,128)S(1)}, f32[128,256]{1,0:T(8,128)S(1)}, u32[]{:S(2)}, u32[]{:S(2)}) collective-permute-start(f32[128,256]{1,0:T(8,128)S(1)} %constant_dynamic-slice_fusion.1), channel_id=1, source_target_pairs={{0,2},{1,3},{2,0},{3,1},{4,6},{5,7},{6,4},{7,5},{8,10},{9,11},{10,... | collective-permute-start | bytes 393224 | tf_op jit(solution)/shard_map/ppermute | solution.py:24
  55.5 3.8 %collective-permute-done.32 = f32[128,256]{1,0:T(8,128)S(1)} collective-permute-done((f32[128,256]{1,0:T(8,128)S(1)}, f32[128,256]{1,0:T(8,128)S(1)}, u32[]{:S(2)}, u32[]{:S(2)}) %collective-permute-start.32) | collective-permute-done | bytes 131104 | tf_op jit(solution)/shard_map/ppermute | solution.py:24
  59.4 3.5 %collective-permute-start.33 = (f32[64,256]{1,0:T(8,128)S(1)}, f32[64,256]{1,0:T(8,128)S(1)}, u32[]{:S(2)}, u32[]{:S(2)}) collective-permute-start(f32[64,256]{1,0:T(8,128)S(1)} %constant_dynamic-slice_fusion), channel_id=1, source_target_pairs={{0,4},{1,5},{2,6},{3,7},{4,0},{5,1},{6,2},{7,3},{8,12},{9,13},{10,... | collective-permute-start | bytes 196616 | tf_op jit(solution)/shard_map/ppermute | solution.py:24
  63.0 4.5 %collective-permute-start.15 = (bf16[128,1024]{1,0:T(8,128)(2,1)S(1)}, bf16[128,1024]{1,0:T(8,128)(2,1)}, u32[]{:S(2)}, u32[]{:S(2)}) collective-permute-start(bf16[128,1024]{1,0:T(8,128)(2,1)S(1)} %pad_maximum_fusion.1), channel_id=1, source_target_pairs={{0,0},{1,1},{2,32},{3,33},{4,64},{5,65},{6,96},{7,97},{8,16},{9,17... | collective-permute-start | bytes 786440 | tf_op jit(solution)/shard_map/ppermute | solution.py:24
  67.7 4.3 %collective-permute-done.34 = f32[64,256]{1,0:T(8,128)S(1)} collective-permute-done((f32[64,256]{1,0:T(8,128)S(1)}, f32[64,256]{1,0:T(8,128)S(1)}, u32[]{:S(2)}, u32[]{:S(2)}) %collective-permute-start.34) | collective-permute-done | bytes 65568 | tf_op jit(solution)/shard_map/ppermute | solution.py:24
  71.9 4.0 %collective-permute-start.37 = (f32[64,256]{1,0:T(8,128)S(1)}, f32[64,256]{1,0:T(8,128)S(1)}, u32[]{:S(2)}, u32[]{:S(2)}) collective-permute-start(f32[64,256]{1,0:T(8,128)S(1)} %add.497), channel_id=1, source_target_pairs={{0,96},{1,97},{2,98},{3,99},{4,100},{5,101},{6,102},{7,103},{8,104... | collective-permute-start | bytes 196616 | tf_op jit(solution)/shard_map/ppermute | solution.py:24
  79.9 2.5 %collective-permute-start.19 = (bf16[128,1024]{1,0:T(8,128)(2,1)}, bf16[128,1024]{1,0:T(8,128)(2,1)}, u32[]{:S(2)}, u32[]{:S(2)}) collective-permute-start(bf16[128,1024]{1,0:T(8,128)(2,1)} %collective-permute-done.15), channel_id=1, source_target_pairs={{0,64},{1,65},{2,66},{3,67},{4,68},{5,69},{6,70},{7,71},{8,72},{9,... | collective-permute-start | bytes 786440 | tf_op jit(solution)/shard_map/ppermute | solution.py:24
  82.4 3.5 %collective-permute-start.38 = (bf16[64,256]{1,0:T(8,128)(2,1)S(1)}, bf16[64,256]{1,0:T(8,128)(2,1)S(1)}, u32[]{:S(2)}, u32[]{:S(2)}) collective-permute-start(bf16[64,256]{1,0:T(8,128)(2,1)S(1)} %add_convert_fusion.2), channel_id=1, source_target_pairs={{0,8},{1,9},{2,10},{3,11},{4,12},{5,13},{6,14},{7,15},{8,0},{9,1},... | collective-permute-start | bytes 98312 | tf_op jit(solution)/shard_map/ppermute | solution.py:24
  86.0 2.0 %collective-permute-start.22 = (bf16[256,1024]{1,0:T(8,128)(2,1)S(1)}, bf16[256,1024]{1,0:T(8,128)(2,1)S(1)}, u32[]{:S(2)}, u32[]{:S(2)}) collective-permute-start(bf16[256,1024]{1,0:T(8,128)(2,1)S(1)} %pad_maximum_fusion.refs_5_), channel_id=1, source_target_pairs={{0,2},{1,3},{2,4},{3,5},{4,6},{5,7},{6,0},{7,1},{8,10},{9,11},{10,... | collective-permute-start | bytes 1572872 | tf_op jit(solution)/shard_map/ppermute | solution.py:24
  92.2 7.6 %collective-permute-done.39 = bf16[64,512]{1,0:T(8,128)(2,1)S(1)} collective-permute-done((bf16[64,512]{1,0:T(8,128)(2,1)}, bf16[64,512]{1,0:T(8,128)(2,1)S(1)}, u32[]{:S(2)}, u32[]{:S(2)}) %collective-permute-start.39) | collective-permute-done | bytes 65568 | tf_op jit(solution)/shard_map/ppermute | solution.py:24
  101.6 2.6 %collective-permute-start.40 = (bf16[128,512]{1,0:T(8,128)(2,1)S(1)}, bf16[128,512]{1,0:T(8,128)(2,1)}, u32[]{:S(2)}, u32[]{:S(2)}) collective-permute-start(bf16[128,512]{1,0:T(8,128)(2,1)S(1)} %maximum_select_fusion.1), channel_id=1, source_target_pairs={{0,2},{1,3},{2,0},{3,1},{4,6},{5,7},{6,4},{7,5},{8,10},{9,11},{10,... | collective-permute-start | bytes 393224 | tf_op jit(solution)/shard_map/ppermute | solution.py:24
  111.7 9.1 %collective-permute-done.18.refs_2_ = bf16[256,1024]{1,0:T(8,128)(2,1)} collective-permute-done((bf16[256,1024]{1,0:T(8,128)(2,1)S(1)}, bf16[256,1024]{1,0:T(8,128)(2,1)}, u32[]{:S(2)}, u32[]{:S(2)}) %collective-permute-start.18) | collective-permute-done | bytes 524320 | tf_op jit(solution)/shard_map/ppermute | solution.py:24
  120.8 3.2 %collective-permute-done.17.refs_1_ = bf16[256,1024]{1,0:T(8,128)(2,1)} collective-permute-done((bf16[256,1024]{1,0:T(8,128)(2,1)S(1)}, bf16[256,1024]{1,0:T(8,128)(2,1)}, u32[]{:S(2)}, u32[]{:S(2)}) %collective-permute-start.17) | collective-permute-done | bytes 524320 | tf_op jit(solution)/shard_map/ppermute | solution.py:24
  126.9 14.0 %shard_map.86 = (f32[2048,1024]{1,0:T(8,128)}, bf16[2048,1024]{1,0:T(8,128)(2,1)}) custom-call(s32[26]{0:T(128)S(1)} %pad_add_fusion.spot, bf16[256,1024]{1,0:T(8,128)(2,1)S(1)} %constant_dynamic-update-slice_fusion.refs_0_, bf16[256,1024]{1,0:T(8,128)(2,1)} %collective-permute-done.17.refs_1_, bf16[256,1024]{1,0:T(8,128)(2,1)} %collective-permute-done.18.refs_2_, ...), custom_call_target="tpu_custom_call" | custom-call | flops 8999999488 | bytes 29360128 | tf_op jit(solution)/shard_map/pallas_call | solution.py:165
  (113 shorter events, 37.0 us)
Async XLA Ops:
  8.5 32.8 %collective-permute-start.9 = (bf16[128,512]{1,0:T(8,128)(2,1)S(1)}, bf16[128,512]{1,0:T(8,128)(2,1)S(1)}, u32[]{:S(2)}, u32[]{:S(2)}) collective-permute-start(bf16[128,512]{1,0:T(8,128)(2,1)S(1)} %get-tuple-element.53), channel_id=1, source_target_pairs={{0,4},{1,5},{2,6},{3,7},{4,0},{5,1},{6,2},{7,3},{8,12},{9,13},{10,... | collective-permute-start | bytes 393224 | tf_op jit(solution)/shard_map/ppermute | solution.py:24
  10.9 29.9 %collective-permute-start.14 = (bf16[128,512]{1,0:T(8,128)(2,1)S(1)}, bf16[128,512]{1,0:T(8,128)(2,1)S(1)}, u32[]{:S(2)}, u32[]{:S(2)}) collective-permute-start(bf16[128,512]{1,0:T(8,128)(2,1)S(1)} %get-tuple-element.54), channel_id=1, source_target_pairs={{0,14},{1,15},{2,8},{3,9},{4,10},{5,11},{6,12},{7,13},{8,6},{9,7},... | collective-permute-start | bytes 393224 | tf_op jit(solution)/shard_map/ppermute | solution.py:24
  15.6 24.6 %collective-permute-start.13 = (bf16[128,512]{1,0:T(8,128)(2,1)S(1)}, bf16[128,512]{1,0:T(8,128)(2,1)S(1)}, u32[]{:S(2)}, u32[]{:S(2)}) collective-permute-start(bf16[128,512]{1,0:T(8,128)(2,1)S(1)} %get-tuple-element.55), channel_id=1, source_target_pairs={{0,12},{1,13},{2,14},{3,15},{4,8},{5,9},{6,10},{7,11},{8,4},{9,5},... | collective-permute-start | bytes 393224 | tf_op jit(solution)/shard_map/ppermute | solution.py:24
  15.6 24.1 %collective-permute-start.12 = (bf16[128,512]{1,0:T(8,128)(2,1)S(1)}, bf16[128,512]{1,0:T(8,128)(2,1)S(1)}, u32[]{:S(2)}, u32[]{:S(2)}) collective-permute-start(bf16[128,512]{1,0:T(8,128)(2,1)S(1)} %get-tuple-element.56), channel_id=1, source_target_pairs={{0,10},{1,11},{2,12},{3,13},{4,14},{5,15},{6,8},{7,9},{8,2},{9,3},... | collective-permute-start | bytes 393224 | tf_op jit(solution)/shard_map/ppermute | solution.py:24
  43.4 8.0 %collective-permute-start.21 = (bf16[128,1024]{1,0:T(8,128)(2,1)S(1)}, bf16[128,1024]{1,0:T(8,128)(2,1)S(1)}, u32[]{:S(2)}, u32[]{:S(2)}) collective-permute-start(bf16[128,1024]{1,0:T(8,128)(2,1)S(1)} %pad_maximum_fusion.1), channel_id=1, source_target_pairs={{0,8},{1,9},{2,10},{3,11},{4,12},{5,13},{6,14},{7,15},{8,0},{9,1},... | collective-permute-start | bytes 786440 | tf_op jit(solution)/shard_map/ppermute | solution.py:24
  59.4 8.2 %collective-permute-start.33 = (f32[64,256]{1,0:T(8,128)S(1)}, f32[64,256]{1,0:T(8,128)S(1)}, u32[]{:S(2)}, u32[]{:S(2)}) collective-permute-start(f32[64,256]{1,0:T(8,128)S(1)} %constant_dynamic-slice_fusion), channel_id=1, source_target_pairs={{0,4},{1,5},{2,6},{3,7},{4,0},{5,1},{6,2},{7,3},{8,12},{9,13},{10,... | collective-permute-start | bytes 196616 | tf_op jit(solution)/shard_map/ppermute | solution.py:24
  62.9 14.3 %collective-permute-start.24 = (bf16[128,1024]{1,0:T(8,128)(2,1)S(1)}, bf16[128,1024]{1,0:T(8,128)(2,1)S(1)}, u32[]{:S(2)}, u32[]{:S(2)}) collective-permute-start(bf16[128,1024]{1,0:T(8,128)(2,1)S(1)} %pad_maximum_fusion.1), channel_id=1, source_target_pairs={{0,4},{1,5},{2,6},{3,7},{4,0},{5,1},{6,2},{7,3},{8,12},{9,13},{10,... | collective-permute-start | bytes 786440 | tf_op jit(solution)/shard_map/ppermute | solution.py:24
  63.0 15.5 %collective-permute-start.15 = (bf16[128,1024]{1,0:T(8,128)(2,1)S(1)}, bf16[128,1024]{1,0:T(8,128)(2,1)}, u32[]{:S(2)}, u32[]{:S(2)}) collective-permute-start(bf16[128,1024]{1,0:T(8,128)(2,1)S(1)} %pad_maximum_fusion.1), channel_id=1, source_target_pairs={{0,0},{1,1},{2,32},{3,33},{4,64},{5,65},{6,96},{7,97},{8,16},{9,17... | collective-permute-start | bytes 786440 | tf_op jit(solution)/shard_map/ppermute | solution.py:24
  71.9 8.0 %collective-permute-start.37 = (f32[64,256]{1,0:T(8,128)S(1)}, f32[64,256]{1,0:T(8,128)S(1)}, u32[]{:S(2)}, u32[]{:S(2)}) collective-permute-start(f32[64,256]{1,0:T(8,128)S(1)} %add.497), channel_id=1, source_target_pairs={{0,96},{1,97},{2,98},{3,99},{4,100},{5,101},{6,102},{7,103},{8,104... | collective-permute-start | bytes 196616 | tf_op jit(solution)/shard_map/ppermute | solution.py:24
  77.2 8.7 %collective-permute-start.29 = (bf16[128,1024]{1,0:T(8,128)(2,1)S(1)}, bf16[128,1024]{1,0:T(8,128)(2,1)S(1)}, u32[]{:S(2)}, u32[]{:S(2)}) collective-permute-start(bf16[128,1024]{1,0:T(8,128)(2,1)S(1)} %collective-permute-done.24.refs_8_), channel_id=1, source_target_pairs={{0,1},{1,0},{2,3},{3,2},{4,5},{5,4},{6,7},{7,6},{8,9},{9,8},{10,11... | collective-permute-start | bytes 786440 | tf_op jit(solution)/shard_map/ppermute | solution.py:24
  78.6 9.4 %collective-permute-start.25 = (bf16[128,1024]{1,0:T(8,128)(2,1)S(1)}, bf16[128,1024]{1,0:T(8,128)(2,1)S(1)}, u32[]{:S(2)}, u32[]{:S(2)}) collective-permute-start(bf16[128,1024]{1,0:T(8,128)(2,1)S(1)} %collective-permute-done.24.refs_8_), channel_id=1, source_target_pairs={{0,8},{1,9},{2,10},{3,11},{4,12},{5,13},{6,14},{7,15},{8,0},{9,1},... | collective-permute-start | bytes 786440 | tf_op jit(solution)/shard_map/ppermute | solution.py:24
  79.9 10.4 %collective-permute-start.19 = (bf16[128,1024]{1,0:T(8,128)(2,1)}, bf16[128,1024]{1,0:T(8,128)(2,1)}, u32[]{:S(2)}, u32[]{:S(2)}) collective-permute-start(bf16[128,1024]{1,0:T(8,128)(2,1)} %collective-permute-done.15), channel_id=1, source_target_pairs={{0,64},{1,65},{2,66},{3,67},{4,68},{5,69},{6,70},{7,71},{8,72},{9,... | collective-permute-start | bytes 786440 | tf_op jit(solution)/shard_map/ppermute | solution.py:24
  85.9 23.1 %collective-permute-start.23 = (bf16[256,1024]{1,0:T(8,128)(2,1)S(1)}, bf16[256,1024]{1,0:T(8,128)(2,1)S(1)}, u32[]{:S(2)}, u32[]{:S(2)}) collective-permute-start(bf16[256,1024]{1,0:T(8,128)(2,1)S(1)} %pad_maximum_fusion.refs_5_), channel_id=1, source_target_pairs={{0,6},{1,7},{2,0},{3,1},{4,2},{5,3},{6,4},{7,5},{8,14},{9,15},{10,... | collective-permute-start | bytes 1572872 | tf_op jit(solution)/shard_map/ppermute | solution.py:24
  86.0 23.8 %collective-permute-start.22 = (bf16[256,1024]{1,0:T(8,128)(2,1)S(1)}, bf16[256,1024]{1,0:T(8,128)(2,1)S(1)}, u32[]{:S(2)}, u32[]{:S(2)}) collective-permute-start(bf16[256,1024]{1,0:T(8,128)(2,1)S(1)} %pad_maximum_fusion.refs_5_), channel_id=1, source_target_pairs={{0,2},{1,3},{2,4},{3,5},{4,6},{5,7},{6,0},{7,1},{8,10},{9,11},{10,... | collective-permute-start | bytes 1572872 | tf_op jit(solution)/shard_map/ppermute | solution.py:24
  88.0 13.5 %collective-permute-start.16 = (bf16[128,1024]{1,0:T(8,128)(2,1)}, bf16[128,1024]{1,0:T(8,128)(2,1)}, u32[]{:S(2)}, u32[]{:S(2)}) collective-permute-start(bf16[128,1024]{1,0:T(8,128)(2,1)} %collective-permute-done.15), channel_id=1, source_target_pairs={{0,16},{1,17},{2,18},{3,19},{4,20},{5,21},{6,22},{7,23},{8,24},{9,... | collective-permute-start | bytes 786440 | tf_op jit(solution)/shard_map/ppermute | solution.py:24
  88.9 12.6 %collective-permute-start.30 = (bf16[128,1024]{1,0:T(8,128)(2,1)S(1)}, bf16[128,1024]{1,0:T(8,128)(2,1)}, u32[]{:S(2)}, u32[]{:S(2)}) collective-permute-start(bf16[128,1024]{1,0:T(8,128)(2,1)S(1)} %collective-permute-done.25.refs_9_), channel_id=1, source_target_pairs={{0,1},{1,0},{2,3},{3,2},{4,5},{5,4},{6,7},{7,6},{8,9},{9,8},{10,11... | collective-permute-start | bytes 786440 | tf_op jit(solution)/shard_map/ppermute | solution.py:24
  90.3 9.6 %collective-permute-start.39 = (bf16[64,512]{1,0:T(8,128)(2,1)}, bf16[64,512]{1,0:T(8,128)(2,1)S(1)}, u32[]{:S(2)}, u32[]{:S(2)}) collective-permute-start(bf16[64,512]{1,0:T(8,128)(2,1)} %maximum_select_fusion.2), channel_id=1, source_target_pairs={{0,4},{1,5},{2,6},{3,7},{4,0},{5,1},{6,2},{7,3},{8,12},{9,13},{10,... | collective-permute-start | bytes 196616 | tf_op jit(solution)/shard_map/ppermute | solution.py:24
  101.4 9.9 %collective-permute-start.26 = (bf16[256,1024]{1,0:T(8,128)(2,1)S(1)}, bf16[256,1024]{1,0:T(8,128)(2,1)}, u32[]{:S(2)}, u32[]{:S(2)}) collective-permute-start(bf16[256,1024]{1,0:T(8,128)(2,1)S(1)} %pad_maximum_fusion.refs_5_), channel_id=1, source_target_pairs={{0,1},{1,0},{2,3},{3,2},{4,5},{5,4},{6,7},{7,6},{8,9},{9,8},{10,11... | collective-permute-start | bytes 1572872 | tf_op jit(solution)/shard_map/ppermute | solution.py:24
  101.6 8.2 %collective-permute-start.40 = (bf16[128,512]{1,0:T(8,128)(2,1)S(1)}, bf16[128,512]{1,0:T(8,128)(2,1)}, u32[]{:S(2)}, u32[]{:S(2)}) collective-permute-start(bf16[128,512]{1,0:T(8,128)(2,1)S(1)} %maximum_select_fusion.1), channel_id=1, source_target_pairs={{0,2},{1,3},{2,0},{3,1},{4,6},{5,7},{6,4},{7,5},{8,10},{9,11},{10,... | collective-permute-start | bytes 393224 | tf_op jit(solution)/shard_map/ppermute | solution.py:24
  107.7 13.1 %collective-permute-start.18 = (bf16[256,1024]{1,0:T(8,128)(2,1)S(1)}, bf16[256,1024]{1,0:T(8,128)(2,1)}, u32[]{:S(2)}, u32[]{:S(2)}) collective-permute-start(bf16[256,1024]{1,0:T(8,128)(2,1)S(1)} %constant_dynamic-update-slice_fusion.refs_0_), channel_id=1, source_target_pairs={{0,96},{1,97},{2,98},{3,99},{4,100},{5,101},{6,102},{7,103},{8,104... | collective-permute-start | bytes 1572872 | tf_op jit(solution)/shard_map/ppermute | solution.py:24
  109.0 15.0 %collective-permute-start.17 = (bf16[256,1024]{1,0:T(8,128)(2,1)S(1)}, bf16[256,1024]{1,0:T(8,128)(2,1)}, u32[]{:S(2)}, u32[]{:S(2)}) collective-permute-start(bf16[256,1024]{1,0:T(8,128)(2,1)S(1)} %constant_dynamic-update-slice_fusion.refs_0_), channel_id=1, source_target_pairs={{0,32},{1,33},{2,34},{3,35},{4,36},{5,37},{6,38},{7,39},{8,40},{9,... | collective-permute-start | bytes 1572872 | tf_op jit(solution)/shard_map/ppermute | solution.py:24
  109.8 14.2 %collective-permute-start.28 = (bf16[256,1024]{1,0:T(8,128)(2,1)S(1)}, bf16[256,1024]{1,0:T(8,128)(2,1)}, u32[]{:S(2)}, u32[]{:S(2)}) collective-permute-start(bf16[256,1024]{1,0:T(8,128)(2,1)S(1)} %collective-permute-done.23.refs_7_), channel_id=1, source_target_pairs={{0,1},{1,0},{2,3},{3,2},{4,5},{5,4},{6,7},{7,6},{8,9},{9,8},{10,11... | collective-permute-start | bytes 1572872 | tf_op jit(solution)/shard_map/ppermute | solution.py:24
  109.8 14.2 %collective-permute-start.27 = (bf16[256,1024]{1,0:T(8,128)(2,1)S(1)}, bf16[256,1024]{1,0:T(8,128)(2,1)}, u32[]{:S(2)}, u32[]{:S(2)}) collective-permute-start(bf16[256,1024]{1,0:T(8,128)(2,1)S(1)} %collective-permute-done.22.refs_6_), channel_id=1, source_target_pairs={{0,1},{1,0},{2,3},{3,2},{4,5},{5,4},{6,7},{7,6},{8,9},{9,8},{10,11... | collective-permute-start | bytes 1572872 | tf_op jit(solution)/shard_map/ppermute | solution.py:24
  111.4 12.7 %collective-permute-start.41 = (bf16[256,512]{1,0:T(8,128)(2,1)S(1)}, bf16[256,512]{1,0:T(8,128)(2,1)S(1)}, u32[]{:S(2)}, u32[]{:S(2)}) collective-permute-start(bf16[256,512]{1,0:T(8,128)(2,1)S(1)} %maximum_select_fusion.refs_15_), channel_id=1, source_target_pairs={{0,1},{1,0},{2,3},{3,2},{4,5},{5,4},{6,7},{7,6},{8,9},{9,8},{10,11... | collective-permute-start | bytes 786440 | tf_op jit(solution)/shard_map/ppermute | solution.py:24
  (22 other events, 144.7 us)
where the time goes:
time: 142 us; the launch traced here: 141 us
  starting transfers between devices  55.2 us (39%)
  waiting for transfers between devices  46.9 us (33%)
  Pallas kernels  14 us (10%)
  local copies, waits for them, and re-layouts  8.83 us (6%)
  matrix products  7.64 us (5%)
  other arithmetic  6.1 us (4%)
  between operations  2.16 us (2%)
    ppermute x35, starting transfers between devices, move(): return lax.ppermute(value, ('row', 'col'), pairs)  55.2 us
    ppermute x35, waiting for transfers between devices, move(): return lax.ppermute(value, ('row', 'col'), pairs)  46.9 us
    pallas_call x1, Pallas kernels, tail(): pl.pallas_call(tail_kernel, grid_spec=pltpu.PrefetchScalarGridSpec(num_sc...  14 us
    dot_general x11, matrix products, mm(): return jnp.dot(a, b, preferred_element_type=F32)  7.38 us
    unnamed x23, local copies, waits for them, and re-layouts  6.02 us
  transfers between devices with their start and end apart: 35, of which 13 were waited for; matrix products, arithmetic and copies ran while one was open for 8% of the time, Pallas kernels for 0%

commit v1 on v0

--- a/solution.py
+++ b/solution.py
@@ -48,10 +48,6 @@
     return lambda x, zl, zh, y, k: (x ^ bit, zl, zh, y, k)
 
 
-def flip_y(bit):
-    return lambda x, zl, zh, y, k: (x, zl, zh, y ^ bit, k)
-
-
 def to_strip(x, zl, zh, y, k):
     zh2 = x // 2
     return x + y, zh ^ zl ^ zh2, zh2, (x % 2) * 2 + zl, k
@@ -59,6 +55,10 @@
 
 def rows(value, start, count):
     return lax.dynamic_slice_in_dim(value, start, count, 0)
+
+
+def put(buffer, piece, start):
+    return lax.dynamic_update_slice_in_dim(buffer, piece, start, 0)
 
 
 def joined(mine, theirs, mine_second, axis):
@@ -258,16 +258,18 @@
     right = lax.dynamic_slice_in_dim(pair, 512 + zh * 256, 256, 1)
     gram = lax.dot_general(fp, right, (((0,), (0,)), ((), ())), preferred_element_type=F32)
     gram = rows(gram, k * 256, 256) + move(rows(gram, (1 - k) * 256, 256), other_core)
-    odd, high = y % 2, y // 2
-    total = rows(gram, odd * 128, 128) + move(rows(gram, (1 - odd) * 128, 128), flip_y(1))
-    total = rows(total, high * 64, 64) + move(rows(total, (1 - high) * 64, 64), flip_y(2))
+    total = rows(gram, y * 64, 64)
+    for step in (1, 2, 3):
+        total = total + move(rows(gram, ((y + step) % 4) * 64, 64), along_y(step))
     total = total + move(total, other_zl)
     one, two, three = [move(total, flip_x(bit)) for bit in (1, 2, 3)]
     total = (total + one) + (two + three)
     low = total.astype(BF)
     low = joined(low, move(low, other_zh), zh, 1)
-    low = joined(low, move(low, flip_y(2)), high, 0)
-    low = joined(low, move(low, flip_y(1)), odd, 0)
+    whole = put(jnp.zeros((256, 512), BF), low, y * 64)
+    for step in (1, 2, 3):
+        whole = put(whole, move(low, along_y(step)), ((y - step) % 4) * 64)
+    low = whole
     grams = [low, move(low, other_core)]
 
     index = lax.iota(jnp.int32, 24)

time: 142 us -> 138 us (0.972)
  local copies, waits for them, and re-layouts: 8.83 us -> 2.1 us
  waiting for transfers between devices: 46.9 us -> 52.9 us
  other arithmetic: 6.1 us -> 3.45 us
  Pallas kernels: 14 us -> 12.2 us
    ppermute x35 -> x37, waiting for transfers between devices: 46.9 us -> 52.9 us  [move(): return lax.ppermute(value, ('row', 'col'), pairs)]
    unnamed x23 -> x9, local copies, waits for them, and re-layouts: 6.02 us -> 0.2 us
    select_n x3 -> x0, other arithmetic: 2.66 us -> none  [joined(): jnp.where(mine_second == 1, jnp.concatenate([theirs, mine], axis), jnp.co...]
    pallas_call x1, Pallas kernels: 14 us -> 12.2 us  [tail(): pl.pallas_call(tail_kernel, grid_spec=pltpu.PrefetchScalarGridSpec(num_sc...]
    ppermute x35 -> x37, starting transfers between devices: 55.2 us -> 55.7 us  [move(): return lax.ppermute(value, ('row', 'col'), pairs)]
  transfers between devices with their start and end apart: 35 -> 37, of which waited for: 13 -> 13; matrix products, arithmetic and copies ran while one was open for 8% -> 5% of each run, Pallas kernels for 0% -> 0%
where the time goes in v1:
time: 138 us; the launch traced here: 137 us
  starting transfers between devices  55.7 us (40%)
  waiting for transfers between devices  52.9 us (38%)
  Pallas kernels  12.2 us (9%)
  matrix products  7.64 us (6%)
  other arithmetic  3.45 us (2%)
  between operations  2.28 us (2%)
  local copies, waits for them, and re-layouts  2.1 us (2%)
    ppermute x37, starting transfers between devices, move(): return lax.ppermute(value, ('row', 'col'), pairs)  55.7 us
    ppermute x37, waiting for transfers between devices, move(): return lax.ppermute(value, ('row', 'col'), pairs)  52.9 us
    pallas_call x1, Pallas kernels, tail(): pl.pallas_call(tail_kernel, grid_spec=pltpu.PrefetchScalarGridSpec(num_sc...  12.2 us
    dot_general x11, matrix products, mm(): return jnp.dot(a, b, preferred_element_type=F32)  7.37 us
  transfers between devices with their start and end apart: 37, of which 13 were waited for; matrix products, arithmetic and copies ran while one was open for 5% of the time, Pallas kernels for 0%

profile of v1, /device:TPU:8, one launch (start us, length us, event | category | flops | bytes accessed | tf_op | source)
XLA Modules:
  0.0 136.5 jit_solution(16669105741443911123)
XLA Ops:
  8.5 2.4 %collective-permute-start.9 = (bf16[128,512]{1,0:T(8,128)(2,1)S(1)}, bf16[128,512]{1,0:T(8,128)(2,1)S(1)}, u32[]{:S(2)}, u32[]{:S(2)}) collective-permute-start(bf16[128,512]{1,0:T(8,128)(2,1)S(1)} %get-tuple-element.55), channel_id=1, source_target_pairs={{0,4},{1,5},{2,6},{3,7},{4,0},{5,1},{6,2},{7,3},{8,12},{9,13},{10,... | collective-permute-start | bytes 393224 | tf_op jit(solution)/shard_map/ppermute | solution.py:24
  10.9 4.7 %collective-permute-start.14 = (bf16[128,512]{1,0:T(8,128)(2,1)S(1)}, bf16[128,512]{1,0:T(8,128)(2,1)S(1)}, u32[]{:S(2)}, u32[]{:S(2)}) collective-permute-start(bf16[128,512]{1,0:T(8,128)(2,1)S(1)} %get-tuple-element.56), channel_id=1, source_target_pairs={{0,14},{1,15},{2,8},{3,9},{4,10},{5,11},{6,12},{7,13},{8,6},{9,7},... | collective-permute-start | bytes 393224 | tf_op jit(solution)/shard_map/ppermute | solution.py:24
  15.6 4.9 %collective-permute-start.12 = (bf16[128,512]{1,0:T(8,128)(2,1)S(1)}, bf16[128,512]{1,0:T(8,128)(2,1)S(1)}, u32[]{:S(2)}, u32[]{:S(2)}) collective-permute-start(bf16[128,512]{1,0:T(8,128)(2,1)S(1)} %get-tuple-element.58), channel_id=1, source_target_pairs={{0,10},{1,11},{2,12},{3,13},{4,14},{5,15},{6,8},{7,9},{8,2},{9,3},... | collective-permute-start | bytes 393224 | tf_op jit(solution)/shard_map/ppermute | solution.py:24
  22.6 5.0 %collective-permute-done.8 = bf16[128,512]{1,0:T(8,128)(2,1)S(1)} collective-permute-done((bf16[128,512]{1,0:T(8,128)(2,1)S(1)}, bf16[128,512]{1,0:T(8,128)(2,1)S(1)}, u32[]{:S(2)}, u32[]{:S(2)}) %collective-permute-start.8) | collective-permute-done | bytes 131104 | tf_op jit(solution)/shard_map/ppermute | solution.py:24
  27.7 2.0 %collective-permute-start.10 = (bf16[128,512]{1,0:T(8,128)(2,1)S(1)}, bf16[128,512]{1,0:T(8,128)(2,1)S(1)}, u32[]{:S(2)}, u32[]{:S(2)}) collective-permute-start(bf16[128,512]{1,0:T(8,128)(2,1)S(1)} %get-tuple-element.60), channel_id=1, source_target_pairs={{0,6},{1,7},{2,0},{3,1},{4,2},{5,3},{6,4},{7,5},{8,14},{9,15},{10,... | collective-permute-start | bytes 393224 | tf_op jit(solution)/shard_map/ppermute | solution.py:24
  30.2 2.4 %collective-permute-done.10 = bf16[128,512]{1,0:T(8,128)(2,1)S(1)} collective-permute-done((bf16[128,512]{1,0:T(8,128)(2,1)S(1)}, bf16[128,512]{1,0:T(8,128)(2,1)S(1)}, u32[]{:S(2)}, u32[]{:S(2)}) %collective-permute-start.10) | collective-permute-done | bytes 131104 | tf_op jit(solution)/shard_map/ppermute | solution.py:24
  32.6 3.2 %collective-permute-start.11 = (bf16[128,512]{1,0:T(8,128)(2,1)S(1)}, bf16[128,512]{1,0:T(8,128)(2,1)S(1)}, u32[]{:S(2)}, u32[]{:S(2)}) collective-permute-start(bf16[128,512]{1,0:T(8,128)(2,1)S(1)} %get-tuple-element.59), channel_id=1, source_target_pairs={{0,8},{1,9},{2,10},{3,11},{4,12},{5,13},{6,14},{7,15},{8,0},{9,1},... | collective-permute-start | bytes 393224 | tf_op jit(solution)/shard_map/ppermute | solution.py:24
  36.4 2.7 %collective-permute-done.11 = bf16[128,512]{1,0:T(8,128)(2,1)S(1)} collective-permute-done((bf16[128,512]{1,0:T(8,128)(2,1)S(1)}, bf16[128,512]{1,0:T(8,128)(2,1)S(1)}, u32[]{:S(2)}, u32[]{:S(2)}) %collective-permute-start.11) | collective-permute-done | bytes 131104 | tf_op jit(solution)/shard_map/ppermute | solution.py:24
  43.4 3.3 %collective-permute-start.21 = (bf16[128,1024]{1,0:T(8,128)(2,1)S(1)}, bf16[128,1024]{1,0:T(8,128)(2,1)S(1)}, u32[]{:S(2)}, u32[]{:S(2)}) collective-permute-start(bf16[128,1024]{1,0:T(8,128)(2,1)S(1)} %pad_maximum_fusion.1), channel_id=1, source_target_pairs={{0,8},{1,9},{2,10},{3,11},{4,12},{5,13},{6,14},{7,15},{8,0},{9,1},... | collective-permute-start | bytes 786440 | tf_op jit(solution)/shard_map/ppermute | solution.py:24
  46.7 4.7 %collective-permute-done.21 = bf16[128,1024]{1,0:T(8,128)(2,1)S(1)} collective-permute-done((bf16[128,1024]{1,0:T(8,128)(2,1)S(1)}, bf16[128,1024]{1,0:T(8,128)(2,1)S(1)}, u32[]{:S(2)}, u32[]{:S(2)}) %collective-permute-start.21) | collective-permute-done | bytes 262176 | tf_op jit(solution)/shard_map/ppermute | solution.py:24
  51.9 3.8 %collective-permute-start.24 = (bf16[128,1024]{1,0:T(8,128)(2,1)S(1)}, bf16[128,1024]{1,0:T(8,128)(2,1)S(1)}, u32[]{:S(2)}, u32[]{:S(2)}) collective-permute-start(bf16[128,1024]{1,0:T(8,128)(2,1)S(1)} %pad_maximum_fusion.1), channel_id=1, source_target_pairs={{0,4},{1,5},{2,6},{3,7},{4,0},{5,1},{6,2},{7,3},{8,12},{9,13},{10,... | collective-permute-start | bytes 786440 | tf_op jit(solution)/shard_map/ppermute | solution.py:24
  55.9 2.0 %collective-permute-start.34 = (f32[64,256]{1,0:T(8,128)S(1)}, f32[64,256]{1,0:T(8,128)S(1)}, u32[]{:S(2)}, u32[]{:S(2)}) collective-permute-start(f32[64,256]{1,0:T(8,128)S(1)} %get-tuple-element.63), channel_id=1, source_target_pairs={{0,6},{1,7},{2,0},{3,1},{4,2},{5,3},{6,4},{7,5},{8,14},{9,15},{10,... | collective-permute-start | bytes 196616 | tf_op jit(solution)/shard_map/ppermute | solution.py:24
  59.3 3.6 %collective-permute-start.15 = (bf16[128,1024]{1,0:T(8,128)(2,1)S(1)}, bf16[128,1024]{1,0:T(8,128)(2,1)S(1)}, u32[]{:S(2)}, u32[]{:S(2)}) collective-permute-start(bf16[128,1024]{1,0:T(8,128)(2,1)S(1)} %pad_maximum_fusion.1), channel_id=1, source_target_pairs={{0,0},{1,1},{2,32},{3,33},{4,64},{5,65},{6,96},{7,97},{8,16},{9,17... | collective-permute-start | bytes 786440 | tf_op jit(solution)/shard_map/ppermute | solution.py:24
  63.7 2.2 %collective-permute-start.25 = (bf16[128,1024]{1,0:T(8,128)(2,1)S(1)}, bf16[128,1024]{1,0:T(8,128)(2,1)S(1)}, u32[]{:S(2)}, u32[]{:S(2)}) collective-permute-start(bf16[128,1024]{1,0:T(8,128)(2,1)S(1)} %collective-permute-done.24.refs_8_), channel_id=1, source_target_pairs={{0,8},{1,9},{2,10},{3,11},{4,12},{5,13},{6,14},{7,15},{8,0},{9,1},... | collective-permute-start | bytes 786440 | tf_op jit(solution)/shard_map/ppermute | solution.py:24
  65.9 5.1 %collective-permute-done.33 = f32[64,256]{1,0:T(8,128)S(1)} collective-permute-done((f32[64,256]{1,0:T(8,128)S(1)}, f32[64,256]{1,0:T(8,128)S(1)}, u32[]{:S(2)}, u32[]{:S(2)}) %collective-permute-start.33) | collective-permute-done | bytes 65568 | tf_op jit(solution)/shard_map/ppermute | solution.py:24
  71.1 7.2 %collective-permute-done.15 = bf16[128,1024]{1,0:T(8,128)(2,1)S(1)} collective-permute-done((bf16[128,1024]{1,0:T(8,128)(2,1)S(1)}, bf16[128,1024]{1,0:T(8,128)(2,1)S(1)}, u32[]{:S(2)}, u32[]{:S(2)}) %collective-permute-start.15) | collective-permute-done | bytes 262176 | tf_op jit(solution)/shard_map/ppermute | solution.py:24
  80.8 2.9 %collective-permute-start.37 = (f32[64,256]{1,0:T(8,128)S(1)}, f32[64,256]{1,0:T(8,128)S(1)}, u32[]{:S(2)}, u32[]{:S(2)}) collective-permute-start(f32[64,256]{1,0:T(8,128)S(1)} %add.519), channel_id=1, source_target_pairs={{0,64},{1,65},{2,66},{3,67},{4,68},{5,69},{6,70},{7,71},{8,72},{9,... | collective-permute-start | bytes 196616 | tf_op jit(solution)/shard_map/ppermute | solution.py:24
  83.8 5.5 %collective-permute-done.38 = f32[64,256]{1,0:T(8,128)S(1)} collective-permute-done((f32[64,256]{1,0:T(8,128)S(1)}, f32[64,256]{1,0:T(8,128)S(1)}, u32[]{:S(2)}, u32[]{:S(2)}) %collective-permute-start.38) | collective-permute-done | bytes 65568 | tf_op jit(solution)/shard_map/ppermute | solution.py:24
  89.3 2.0 %collective-permute-start.22 = (bf16[256,1024]{1,0:T(8,128)(2,1)S(1)}, bf16[256,1024]{1,0:T(8,128)(2,1)S(1)}, u32[]{:S(2)}, u32[]{:S(2)}) collective-permute-start(bf16[256,1024]{1,0:T(8,128)(2,1)S(1)} %pad_maximum_fusion.refs_5_), channel_id=1, source_target_pairs={{0,2},{1,3},{2,4},{3,5},{4,6},{5,7},{6,0},{7,1},{8,10},{9,11},{10,... | collective-permute-start | bytes 1572872 | tf_op jit(solution)/shard_map/ppermute | solution.py:24
  92.7 7.4 %collective-permute-done.39 = bf16[64,256]{1,0:T(8,128)(2,1)S(1)} collective-permute-done((bf16[64,256]{1,0:T(8,128)(2,1)S(1)}, bf16[64,256]{1,0:T(8,128)(2,1)S(1)}, u32[]{:S(2)}, u32[]{:S(2)}) %collective-permute-start.39) | collective-permute-done | bytes 32800 | tf_op jit(solution)/shard_map/ppermute | solution.py:24
  101.7 2.7 %collective-permute-start.41 = (bf16[64,512]{1,0:T(8,128)(2,1)S(1)}, bf16[64,512]{1,0:T(8,128)(2,1)S(1)}, u32[]{:S(2)}, u32[]{:S(2)}) collective-permute-start(bf16[64,512]{1,0:T(8,128)(2,1)S(1)} %get-tuple-element.31), channel_id=1, source_target_pairs={{0,4},{1,5},{2,6},{3,7},{4,0},{5,1},{6,2},{7,3},{8,12},{9,13},{10,... | collective-permute-start | bytes 196616 | tf_op jit(solution)/shard_map/ppermute | solution.py:24
  105.0 4.4 %collective-permute-start.42 = (bf16[64,512]{1,0:T(8,128)(2,1)S(1)}, bf16[64,512]{1,0:T(8,128)(2,1)S(1)}, u32[]{:S(2)}, u32[]{:S(2)}) collective-permute-start(bf16[64,512]{1,0:T(8,128)(2,1)S(1)} %get-tuple-element.31), channel_id=1, source_target_pairs={{0,6},{1,7},{2,0},{3,1},{4,2},{5,3},{6,4},{7,5},{8,14},{9,15},{10,... | collective-permute-start | bytes 196616 | tf_op jit(solution)/shard_map/ppermute | solution.py:24
  112.7 10.0 %collective-permute-done.18.refs_2_ = bf16[256,1024]{1,0:T(8,128)(2,1)S(1)} collective-permute-done((bf16[256,1024]{1,0:T(8,128)(2,1)S(1)}, bf16[256,1024]{1,0:T(8,128)(2,1)S(1)}, u32[]{:S(2)}, u32[]{:S(2)}) %collective-permute-start.18) | collective-permute-done | bytes 524320 | tf_op jit(solution)/shard_map/ppermute | solution.py:24
  124.1 12.2 %shard_map.86 = (f32[2048,1024]{1,0:T(8,128)}, bf16[2048,1024]{1,0:T(8,128)(2,1)}) custom-call(s32[26]{0:T(128)S(1)} %pad_add_fusion.spot, bf16[256,1024]{1,0:T(8,128)(2,1)S(1)} %constant_dynamic-update-slice_fusion.refs_0_, bf16[256,1024]{1,0:T(8,128)(2,1)S(1)} %collective-permute-done.17.refs_1_, bf16[256,1024]{1,0:T(8,128)(2,1)S(1)} %collective-permute-done.18.refs_2_, ...), custom_call_target="tpu_custom_call" | custom-call | flops 8999999488 | bytes 29360128 | tf_op jit(solution)/shard_map/pallas_call | solution.py:165
  (103 shorter events, 28.0 us)
Async XLA Ops:
  8.5 32.8 %collective-permute-start.9 = (bf16[128,512]{1,0:T(8,128)(2,1)S(1)}, bf16[128,512]{1,0:T(8,128)(2,1)S(1)}, u32[]{:S(2)}, u32[]{:S(2)}) collective-permute-start(bf16[128,512]{1,0:T(8,128)(2,1)S(1)} %get-tuple-element.55), channel_id=1, source_target_pairs={{0,4},{1,5},{2,6},{3,7},{4,0},{5,1},{6,2},{7,3},{8,12},{9,13},{10,... | collective-permute-start | bytes 393224 | tf_op jit(solution)/shard_map/ppermute | solution.py:24
  10.9 29.9 %collective-permute-start.14 = (bf16[128,512]{1,0:T(8,128)(2,1)S(1)}, bf16[128,512]{1,0:T(8,128)(2,1)S(1)}, u32[]{:S(2)}, u32[]{:S(2)}) collective-permute-start(bf16[128,512]{1,0:T(8,128)(2,1)S(1)} %get-tuple-element.56), channel_id=1, source_target_pairs={{0,14},{1,15},{2,8},{3,9},{4,10},{5,11},{6,12},{7,13},{8,6},{9,7},... | collective-permute-start | bytes 393224 | tf_op jit(solution)/shard_map/ppermute | solution.py:24
  15.6 24.6 %collective-permute-start.13 = (bf16[128,512]{1,0:T(8,128)(2,1)S(1)}, bf16[128,512]{1,0:T(8,128)(2,1)S(1)}, u32[]{:S(2)}, u32[]{:S(2)}) collective-permute-start(bf16[128,512]{1,0:T(8,128)(2,1)S(1)} %get-tuple-element.57), channel_id=1, source_target_pairs={{0,12},{1,13},{2,14},{3,15},{4,8},{5,9},{6,10},{7,11},{8,4},{9,5},... | collective-permute-start | bytes 393224 | tf_op jit(solution)/shard_map/ppermute | solution.py:24
  15.6 24.1 %collective-permute-start.12 = (bf16[128,512]{1,0:T(8,128)(2,1)S(1)}, bf16[128,512]{1,0:T(8,128)(2,1)S(1)}, u32[]{:S(2)}, u32[]{:S(2)}) collective-permute-start(bf16[128,512]{1,0:T(8,128)(2,1)S(1)} %get-tuple-element.58), channel_id=1, source_target_pairs={{0,10},{1,11},{2,12},{3,13},{4,14},{5,15},{6,8},{7,9},{8,2},{9,3},... | collective-permute-start | bytes 393224 | tf_op jit(solution)/shard_map/ppermute | solution.py:24
  51.9 11.0 %collective-permute-start.24 = (bf16[128,1024]{1,0:T(8,128)(2,1)S(1)}, bf16[128,1024]{1,0:T(8,128)(2,1)S(1)}, u32[]{:S(2)}, u32[]{:S(2)}) collective-permute-start(bf16[128,1024]{1,0:T(8,128)(2,1)S(1)} %pad_maximum_fusion.1), channel_id=1, source_target_pairs={{0,4},{1,5},{2,6},{3,7},{4,0},{5,1},{6,2},{7,3},{8,12},{9,13},{10,... | collective-permute-start | bytes 786440 | tf_op jit(solution)/shard_map/ppermute | solution.py:24
  55.9 10.0 %collective-permute-start.34 = (f32[64,256]{1,0:T(8,128)S(1)}, f32[64,256]{1,0:T(8,128)S(1)}, u32[]{:S(2)}, u32[]{:S(2)}) collective-permute-start(f32[64,256]{1,0:T(8,128)S(1)} %get-tuple-element.63), channel_id=1, source_target_pairs={{0,6},{1,7},{2,0},{3,1},{4,2},{5,3},{6,4},{7,5},{8,14},{9,15},{10,... | collective-permute-start | bytes 196616 | tf_op jit(solution)/shard_map/ppermute | solution.py:24
  57.9 13.2 %collective-permute-start.33 = (f32[64,256]{1,0:T(8,128)S(1)}, f32[64,256]{1,0:T(8,128)S(1)}, u32[]{:S(2)}, u32[]{:S(2)}) collective-permute-start(f32[64,256]{1,0:T(8,128)S(1)} %get-tuple-element.64), channel_id=1, source_target_pairs={{0,4},{1,5},{2,6},{3,7},{4,0},{5,1},{6,2},{7,3},{8,12},{9,13},{10,... | collective-permute-start | bytes 196616 | tf_op jit(solution)/shard_map/ppermute | solution.py:24
  59.3 19.0 %collective-permute-start.15 = (bf16[128,1024]{1,0:T(8,128)(2,1)S(1)}, bf16[128,1024]{1,0:T(8,128)(2,1)S(1)}, u32[]{:S(2)}, u32[]{:S(2)}) collective-permute-start(bf16[128,1024]{1,0:T(8,128)(2,1)S(1)} %pad_maximum_fusion.1), channel_id=1, source_target_pairs={{0,0},{1,1},{2,32},{3,33},{4,64},{5,65},{6,96},{7,97},{8,16},{9,17... | collective-permute-start | bytes 786440 | tf_op jit(solution)/shard_map/ppermute | solution.py:24
  62.9 17.9 %collective-permute-start.29 = (bf16[128,1024]{1,0:T(8,128)(2,1)S(1)}, bf16[128,1024]{1,0:T(8,128)(2,1)S(1)}, u32[]{:S(2)}, u32[]{:S(2)}) collective-permute-start(bf16[128,1024]{1,0:T(8,128)(2,1)S(1)} %collective-permute-done.24.refs_8_), channel_id=1, source_target_pairs={{0,1},{1,0},{2,3},{3,2},{4,5},{5,4},{6,7},{7,6},{8,9},{9,8},{10,11... | collective-permute-start | bytes 786440 | tf_op jit(solution)/shard_map/ppermute | solution.py:24
  63.7 20.0 %collective-permute-start.25 = (bf16[128,1024]{1,0:T(8,128)(2,1)S(1)}, bf16[128,1024]{1,0:T(8,128)(2,1)S(1)}, u32[]{:S(2)}, u32[]{:S(2)}) collective-permute-start(bf16[128,1024]{1,0:T(8,128)(2,1)S(1)} %collective-permute-done.24.refs_8_), channel_id=1, source_target_pairs={{0,8},{1,9},{2,10},{3,11},{4,12},{5,13},{6,14},{7,15},{8,0},{9,1},... | collective-permute-start | bytes 786440 | tf_op jit(solution)/shard_map/ppermute | solution.py:24
  78.3 13.0 %collective-permute-start.19 = (bf16[128,1024]{1,0:T(8,128)(2,1)S(1)}, bf16[128,1024]{1,0:T(8,128)(2,1)S(1)}, u32[]{:S(2)}, u32[]{:S(2)}) collective-permute-start(bf16[128,1024]{1,0:T(8,128)(2,1)S(1)} %collective-permute-done.15), channel_id=1, source_target_pairs={{0,64},{1,65},{2,66},{3,67},{4,68},{5,69},{6,70},{7,71},{8,72},{9,... | collective-permute-start | bytes 786440 | tf_op jit(solution)/shard_map/ppermute | solution.py:24
  79.3 12.1 %collective-permute-start.16 = (bf16[128,1024]{1,0:T(8,128)(2,1)S(1)}, bf16[128,1024]{1,0:T(8,128)(2,1)S(1)}, u32[]{:S(2)}, u32[]{:S(2)}) collective-permute-start(bf16[128,1024]{1,0:T(8,128)(2,1)S(1)} %collective-permute-done.15), channel_id=1, source_target_pairs={{0,16},{1,17},{2,18},{3,19},{4,20},{5,21},{6,22},{7,23},{8,24},{9,... | collective-permute-start | bytes 786440 | tf_op jit(solution)/shard_map/ppermute | solution.py:24
  79.3 9.9 %collective-permute-start.38 = (f32[64,256]{1,0:T(8,128)S(1)}, f32[64,256]{1,0:T(8,128)S(1)}, u32[]{:S(2)}, u32[]{:S(2)}) collective-permute-start(f32[64,256]{1,0:T(8,128)S(1)} %add.519), channel_id=1, source_target_pairs={{0,96},{1,97},{2,98},{3,99},{4,100},{5,101},{6,102},{7,103},{8,104... | collective-permute-start | bytes 196616 | tf_op jit(solution)/shard_map/ppermute | solution.py:24
  89.3 20.1 %collective-permute-start.23 = (bf16[256,1024]{1,0:T(8,128)(2,1)S(1)}, bf16[256,1024]{1,0:T(8,128)(2,1)S(1)}, u32[]{:S(2)}, u32[]{:S(2)}) collective-permute-start(bf16[256,1024]{1,0:T(8,128)(2,1)S(1)} %pad_maximum_fusion.refs_5_), channel_id=1, source_target_pairs={{0,6},{1,7},{2,0},{3,1},{4,2},{5,3},{6,4},{7,5},{8,14},{9,15},{10,... | collective-permute-start | bytes 1572872 | tf_op jit(solution)/shard_map/ppermute | solution.py:24
  89.3 20.5 %collective-permute-start.22 = (bf16[256,1024]{1,0:T(8,128)(2,1)S(1)}, bf16[256,1024]{1,0:T(8,128)(2,1)S(1)}, u32[]{:S(2)}, u32[]{:S(2)}) collective-permute-start(bf16[256,1024]{1,0:T(8,128)(2,1)S(1)} %pad_maximum_fusion.refs_5_), channel_id=1, source_target_pairs={{0,2},{1,3},{2,4},{3,5},{4,6},{5,7},{6,0},{7,1},{8,10},{9,11},{10,... | collective-permute-start | bytes 1572872 | tf_op jit(solution)/shard_map/ppermute | solution.py:24
  91.3 8.8 %collective-permute-start.30 = (bf16[128,1024]{1,0:T(8,128)(2,1)S(1)}, bf16[128,1024]{1,0:T(8,128)(2,1)S(1)}, u32[]{:S(2)}, u32[]{:S(2)}) collective-permute-start(bf16[128,1024]{1,0:T(8,128)(2,1)S(1)} %collective-permute-done.25.refs_9_), channel_id=1, source_target_pairs={{0,1},{1,0},{2,3},{3,2},{4,5},{5,4},{6,7},{7,6},{8,9},{9,8},{10,11... | collective-permute-start | bytes 786440 | tf_op jit(solution)/shard_map/ppermute | solution.py:24
  91.4 10.3 %collective-permute-start.20 = (bf16[128,1024]{1,0:T(8,128)(2,1)S(1)}, bf16[128,1024]{1,0:T(8,128)(2,1)S(1)}, u32[]{:S(2)}, u32[]{:S(2)}) collective-permute-start(bf16[128,1024]{1,0:T(8,128)(2,1)S(1)} %collective-permute-done.19.refs_3_), channel_id=1, source_target_pairs={{0,16},{1,17},{2,18},{3,19},{4,20},{5,21},{6,22},{7,23},{8,24},{9,... | collective-permute-start | bytes 786440 | tf_op jit(solution)/shard_map/ppermute | solution.py:24
  100.1 12.0 %collective-permute-start.26 = (bf16[256,1024]{1,0:T(8,128)(2,1)S(1)}, bf16[256,1024]{1,0:T(8,128)(2,1)S(1)}, u32[]{:S(2)}, u32[]{:S(2)}) collective-permute-start(bf16[256,1024]{1,0:T(8,128)(2,1)S(1)} %pad_maximum_fusion.refs_5_), channel_id=1, source_target_pairs={{0,1},{1,0},{2,3},{3,2},{4,5},{5,4},{6,7},{7,6},{8,9},{9,8},{10,11... | collective-permute-start | bytes 1572872 | tf_op jit(solution)/shard_map/ppermute | solution.py:24
  101.7 9.8 %collective-permute-start.41 = (bf16[64,512]{1,0:T(8,128)(2,1)S(1)}, bf16[64,512]{1,0:T(8,128)(2,1)S(1)}, u32[]{:S(2)}, u32[]{:S(2)}) collective-permute-start(bf16[64,512]{1,0:T(8,128)(2,1)S(1)} %get-tuple-element.31), channel_id=1, source_target_pairs={{0,4},{1,5},{2,6},{3,7},{4,0},{5,1},{6,2},{7,3},{8,12},{9,13},{10,... | collective-permute-start | bytes 196616 | tf_op jit(solution)/shard_map/ppermute | solution.py:24
  109.4 13.3 %collective-permute-start.18 = (bf16[256,1024]{1,0:T(8,128)(2,1)S(1)}, bf16[256,1024]{1,0:T(8,128)(2,1)S(1)}, u32[]{:S(2)}, u32[]{:S(2)}) collective-permute-start(bf16[256,1024]{1,0:T(8,128)(2,1)S(1)} %constant_dynamic-update-slice_fusion.refs_0_), channel_id=1, source_target_pairs={{0,96},{1,97},{2,98},{3,99},{4,100},{5,101},{6,102},{7,103},{8,104... | collective-permute-start | bytes 1572872 | tf_op jit(solution)/shard_map/ppermute | solution.py:24
  109.7 14.4 %collective-permute-start.17 = (bf16[256,1024]{1,0:T(8,128)(2,1)S(1)}, bf16[256,1024]{1,0:T(8,128)(2,1)S(1)}, u32[]{:S(2)}, u32[]{:S(2)}) collective-permute-start(bf16[256,1024]{1,0:T(8,128)(2,1)S(1)} %constant_dynamic-update-slice_fusion.refs_0_), channel_id=1, source_target_pairs={{0,32},{1,33},{2,34},{3,35},{4,36},{5,37},{6,38},{7,39},{8,40},{9,... | collective-permute-start | bytes 1572872 | tf_op jit(solution)/shard_map/ppermute | solution.py:24
  111.5 12.7 %collective-permute-start.28 = (bf16[256,1024]{1,0:T(8,128)(2,1)S(1)}, bf16[256,1024]{1,0:T(8,128)(2,1)S(1)}, u32[]{:S(2)}, u32[]{:S(2)}) collective-permute-start(bf16[256,1024]{1,0:T(8,128)(2,1)S(1)} %collective-permute-done.23.refs_7_), channel_id=1, source_target_pairs={{0,1},{1,0},{2,3},{3,2},{4,5},{5,4},{6,7},{7,6},{8,9},{9,8},{10,11... | collective-permute-start | bytes 1572872 | tf_op jit(solution)/shard_map/ppermute | solution.py:24
  111.5 12.7 %collective-permute-start.27 = (bf16[256,1024]{1,0:T(8,128)(2,1)S(1)}, bf16[256,1024]{1,0:T(8,128)(2,1)S(1)}, u32[]{:S(2)}, u32[]{:S(2)}) collective-permute-start(bf16[256,1024]{1,0:T(8,128)(2,1)S(1)} %collective-permute-done.22.refs_6_), channel_id=1, source_target_pairs={{0,1},{1,0},{2,3},{3,2},{4,5},{5,4},{6,7},{7,6},{8,9},{9,8},{10,11... | collective-permute-start | bytes 1572872 | tf_op jit(solution)/shard_map/ppermute | solution.py:24
  112.0 12.1 %collective-permute-start.43 = (bf16[256,512]{1,0:T(8,128)(2,1)S(1)}, bf16[256,512]{1,0:T(8,128)(2,1)S(1)}, u32[]{:S(2)}, u32[]{:S(2)}) collective-permute-start(bf16[256,512]{1,0:T(8,128)(2,1)S(1)} %constant_dynamic-update-slice_fusion.2.refs_15_), channel_id=1, source_target_pairs={{0,1},{1,0},{2,3},{3,2},{4,5},{5,4},{6,7},{7,6},{8,9},{9,8},{10,11... | collective-permute-start | bytes 786440 | tf_op jit(solution)/shard_map/ppermute | solution.py:24
  (17 other events, 133.3 us)

commit v2 on v1

--- a/solution.py
+++ b/solution.py
@@ -57,10 +57,6 @@
     return lax.dynamic_slice_in_dim(value, start, count, 0)
 
 
-def put(buffer, piece, start):
-    return lax.dynamic_update_slice_in_dim(buffer, piece, start, 0)
-
-
 def joined(mine, theirs, mine_second, axis):
     return jnp.where(
         mine_second == 1,
@@ -95,14 +91,15 @@
 
     def fetch(i):
         if i >= 24:
-            source, target, height = pieces[15 + i - 24], gram_here, 256
+            source = pieces[15 + (i - 24) // 4].at[pl.ds(i % 4 * 64, 64)]
+            target, height = gram_here, 64
         else:
             group, half = i // 8, i % 8
             source = pieces[group * 5 + (half // 2 if half < 6 else half - 3)]
             if half < 6:
                 source = source.at[pl.ds(half % 2 * 128, 128)]
             target, height = cols if group == 0 else block, 128
-        at = pl.ds(pl.multiple_of(spot[i] * 128, 128), height)
+        at = pl.ds(pl.multiple_of(spot[i] * 64, height), height)
         return pltpu.make_async_copy(source, target.at[at], piece_sem.at[i])
 
     def rows_of(i):
@@ -123,7 +120,7 @@
 
     constants = pltpu.make_async_copy(inverses.at[1], inverse_here, fixed_sem)
     constants.start()
-    early = (*range(8), 24, 25)
+    early = (*range(8), *range(24, 32))
     for i in early:
         fetch(i).start()
     for i in range(8, 24):
@@ -177,7 +174,7 @@
                 pltpu.VMEM((2048, 1024), F32),
                 pltpu.VMEM((512, 512), BF),
                 pltpu.VMEM((512, 512), BF),
-                pltpu.SemaphoreType.DMA((26,)),
+                pltpu.SemaphoreType.DMA((32,)),
                 pltpu.SemaphoreType.DMA,
                 pltpu.SemaphoreType.DMA((SLABS,)),
                 pltpu.SemaphoreType.DMA((SLABS,)),
@@ -266,10 +263,8 @@
     total = (total + one) + (two + three)
     low = total.astype(BF)
     low = joined(low, move(low, other_zh), zh, 1)
-    whole = put(jnp.zeros((256, 512), BF), low, y * 64)
-    for step in (1, 2, 3):
-        whole = put(whole, move(low, along_y(step)), ((y - step) % 4) * 64)
-    low = whole
+    ring = [low] + [move(low, along_y(step)) for step in (1, 2, 3)]
+    low = jnp.concatenate(ring, axis=0)
     grams = [low, move(low, other_core)]
 
     index = lax.iota(jnp.int32, 24)
@@ -279,7 +274,9 @@
     base = jnp.where(kind == 0, x - first, y)
     spot = (base - hop) % 4 * 2 + lower
     spot += jnp.where(kind == 0, 0, jnp.where(kind == 1, k, 1 - k)) * 8
-    spot = jnp.concatenate([spot, jnp.stack([k, 1 - k]) * 2])
+    chunk = lax.iota(jnp.int32, 8)
+    chunk = jnp.where(chunk < 4, k, 1 - k) * 4 + (y - chunk) % 4
+    spot = jnp.concatenate([spot * 2, chunk])
     return tail(spot, strips + near + far + grams, inverses, signed[None, :], trailing)
 
 

time: 138 us -> 144 us (1.043)
  local copies, waits for them, and re-layouts: 2.1 us -> 10.3 us
  waiting for transfers between devices: 52.9 us -> 48.9 us
    unnamed x9 -> x31, local copies, waits for them, and re-layouts: 0.2 us -> 7.49 us
    ppermute x37, waiting for transfers between devices: 52.9 us -> 48.9 us  [move(): return lax.ppermute(value, ('row', 'col'), pairs)]
  transfers between devices with their start and end apart: 37 -> 37, of which waited for: 13 -> 13; matrix products, arithmetic and copies ran while one was open for 5% -> 7% of each run, Pallas kernels for 0% -> 0%
where the time goes in v2:
time: 144 us; the launch traced here: 142 us
  starting transfers between devices  55.3 us (38%)
  waiting for transfers between devices  48.9 us (34%)
  Pallas kernels  13 us (9%)
  local copies, waits for them, and re-layouts  10.3 us (7%)
  matrix products  7.65 us (5%)
  other arithmetic  4.27 us (3%)
  between operations  2.26 us (2%)
    ppermute x37, starting transfers between devices, move(): return lax.ppermute(value, ('row', 'col'), pairs)  55.3 us
    ppermute x37, waiting for transfers between devices, move(): return lax.ppermute(value, ('row', 'col'), pairs)  48.9 us
    pallas_call x1, Pallas kernels, tail(): pl.pallas_call(tail_kernel, grid_spec=pltpu.PrefetchScalarGridSpec(num_sc...  13 us
    unnamed x31, local copies, waits for them, and re-layouts  7.49 us
    dot_general x11, matrix products, mm(): return jnp.dot(a, b, preferred_element_type=F32)  7.38 us
  transfers between devices with their start and end apart: 37, of which 13 were waited for; matrix products, arithmetic and copies ran while one was open for 7% of the time, Pallas kernels for 0%

profile of v2, /device:TPU:8, one launch (start us, length us, event | category | flops | bytes accessed | tf_op | source)
XLA Modules:
  0.0 141.9 jit_solution(70459259917547085)
XLA Ops:
  8.6 2.4 %collective-permute-start.9 = (bf16[128,512]{1,0:T(8,128)(2,1)S(1)}, bf16[128,512]{1,0:T(8,128)(2,1)S(1)}, u32[]{:S(2)}, u32[]{:S(2)}) collective-permute-start(bf16[128,512]{1,0:T(8,128)(2,1)S(1)} %get-tuple-element.53), channel_id=1, source_target_pairs={{0,4},{1,5},{2,6},{3,7},{4,0},{5,1},{6,2},{7,3},{8,12},{9,13},{10,... | collective-permute-start | bytes 393224 | tf_op jit(solution)/shard_map/ppermute | solution.py:24
  10.9 4.7 %collective-permute-start.14 = (bf16[128,512]{1,0:T(8,128)(2,1)S(1)}, bf16[128,512]{1,0:T(8,128)(2,1)S(1)}, u32[]{:S(2)}, u32[]{:S(2)}) collective-permute-start(bf16[128,512]{1,0:T(8,128)(2,1)S(1)} %get-tuple-element.54), channel_id=1, source_target_pairs={{0,14},{1,15},{2,8},{3,9},{4,10},{5,11},{6,12},{7,13},{8,6},{9,7},... | collective-permute-start | bytes 393224 | tf_op jit(solution)/shard_map/ppermute | solution.py:24
  15.6 4.9 %collective-permute-start.12 = (bf16[128,512]{1,0:T(8,128)(2,1)S(1)}, bf16[128,512]{1,0:T(8,128)(2,1)S(1)}, u32[]{:S(2)}, u32[]{:S(2)}) collective-permute-start(bf16[128,512]{1,0:T(8,128)(2,1)S(1)} %get-tuple-element.56), channel_id=1, source_target_pairs={{0,10},{1,11},{2,12},{3,13},{4,14},{5,15},{6,8},{7,9},{8,2},{9,3},... | collective-permute-start | bytes 393224 | tf_op jit(solution)/shard_map/ppermute | solution.py:24
  22.6 5.1 %collective-permute-done.8 = bf16[128,512]{1,0:T(8,128)(2,1)S(1)} collective-permute-done((bf16[128,512]{1,0:T(8,128)(2,1)S(1)}, bf16[128,512]{1,0:T(8,128)(2,1)S(1)}, u32[]{:S(2)}, u32[]{:S(2)}) %collective-permute-start.8) | collective-permute-done | bytes 131104 | tf_op jit(solution)/shard_map/ppermute | solution.py:24
  30.2 2.4 %collective-permute-done.10 = bf16[128,512]{1,0:T(8,128)(2,1)S(1)} collective-permute-done((bf16[128,512]{1,0:T(8,128)(2,1)S(1)}, bf16[128,512]{1,0:T(8,128)(2,1)S(1)}, u32[]{:S(2)}, u32[]{:S(2)}) %collective-permute-start.10) | collective-permute-done | bytes 131104 | tf_op jit(solution)/shard_map/ppermute | solution.py:24
  32.7 3.2 %collective-permute-start.11 = (bf16[128,512]{1,0:T(8,128)(2,1)S(1)}, bf16[128,512]{1,0:T(8,128)(2,1)S(1)}, u32[]{:S(2)}, u32[]{:S(2)}) collective-permute-start(bf16[128,512]{1,0:T(8,128)(2,1)S(1)} %get-tuple-element.57), channel_id=1, source_target_pairs={{0,8},{1,9},{2,10},{3,11},{4,12},{5,13},{6,14},{7,15},{8,0},{9,1},... | collective-permute-start | bytes 393224 | tf_op jit(solution)/shard_map/ppermute | solution.py:24
  36.4 2.7 %collective-permute-done.11 = bf16[128,512]{1,0:T(8,128)(2,1)S(1)} collective-permute-done((bf16[128,512]{1,0:T(8,128)(2,1)S(1)}, bf16[128,512]{1,0:T(8,128)(2,1)S(1)}, u32[]{:S(2)}, u32[]{:S(2)}) %collective-permute-start.11) | collective-permute-done | bytes 131104 | tf_op jit(solution)/shard_map/ppermute | solution.py:24
  43.5 3.3 %collective-permute-start.21 = (bf16[128,1024]{1,0:T(8,128)(2,1)S(1)}, bf16[128,1024]{1,0:T(8,128)(2,1)S(1)}, u32[]{:S(2)}, u32[]{:S(2)}) collective-permute-start(bf16[128,1024]{1,0:T(8,128)(2,1)S(1)} %pad_maximum_fusion.1), channel_id=1, source_target_pairs={{0,8},{1,9},{2,10},{3,11},{4,12},{5,13},{6,14},{7,15},{8,0},{9,1},... | collective-permute-start | bytes 786440 | tf_op jit(solution)/shard_map/ppermute | solution.py:24
  46.7 4.7 %collective-permute-done.21 = bf16[128,1024]{1,0:T(8,128)(2,1)S(1)} collective-permute-done((bf16[128,1024]{1,0:T(8,128)(2,1)S(1)}, bf16[128,1024]{1,0:T(8,128)(2,1)S(1)}, u32[]{:S(2)}, u32[]{:S(2)}) %collective-permute-start.21) | collective-permute-done | bytes 262176 | tf_op jit(solution)/shard_map/ppermute | solution.py:24
  51.9 3.8 %collective-permute-start.24 = (bf16[128,1024]{1,0:T(8,128)(2,1)S(1)}, bf16[128,1024]{1,0:T(8,128)(2,1)S(1)}, u32[]{:S(2)}, u32[]{:S(2)}) collective-permute-start(bf16[128,1024]{1,0:T(8,128)(2,1)S(1)} %pad_maximum_fusion.1), channel_id=1, source_target_pairs={{0,4},{1,5},{2,6},{3,7},{4,0},{5,1},{6,2},{7,3},{8,12},{9,13},{10,... | collective-permute-start | bytes 786440 | tf_op jit(solution)/shard_map/ppermute | solution.py:24
  58.0 3.1 %collective-permute-start.32 = (f32[64,256]{1,0:T(8,128)S(1)}, f32[64,256]{1,0:T(8,128)S(1)}, u32[]{:S(2)}, u32[]{:S(2)}) collective-permute-start(f32[64,256]{1,0:T(8,128)S(1)} %get-tuple-element.60), channel_id=1, source_target_pairs={{0,2},{1,3},{2,4},{3,5},{4,6},{5,7},{6,0},{7,1},{8,10},{9,11},{10,... | collective-permute-start | bytes 196616 | tf_op jit(solution)/shard_map/ppermute | solution.py:24
  61.1 2.4 %collective-permute-start.33 = (f32[64,256]{1,0:T(8,128)S(1)}, f32[64,256]{1,0:T(8,128)S(1)}, u32[]{:S(2)}, u32[]{:S(2)}) collective-permute-start(f32[64,256]{1,0:T(8,128)S(1)} %get-tuple-element.62), channel_id=1, source_target_pairs={{0,4},{1,5},{2,6},{3,7},{4,0},{5,1},{6,2},{7,3},{8,12},{9,13},{10,... | collective-permute-start | bytes 196616 | tf_op jit(solution)/shard_map/ppermute | solution.py:24
  63.5 5.0 %collective-permute-done.24.refs_8_ = bf16[128,1024]{1,0:T(8,128)(2,1)S(1)} collective-permute-done((bf16[128,1024]{1,0:T(8,128)(2,1)S(1)}, bf16[128,1024]{1,0:T(8,128)(2,1)S(1)}, u32[]{:S(2)}, u32[]{:S(2)}) %collective-permute-start.24) | collective-permute-done | bytes 262176 | tf_op jit(solution)/shard_map/ppermute | solution.py:24
  68.5 2.4 %collective-permute-done.15 = bf16[128,1024]{1,0:T(8,128)(2,1)} collective-permute-done((bf16[128,1024]{1,0:T(8,128)(2,1)S(1)}, bf16[128,1024]{1,0:T(8,128)(2,1)}, u32[]{:S(2)}, u32[]{:S(2)}) %collective-permute-start.15) | collective-permute-done | bytes 262176 | tf_op jit(solution)/shard_map/ppermute | solution.py:24
  72.7 2.3 %collective-permute-start.19 = (bf16[128,1024]{1,0:T(8,128)(2,1)}, bf16[128,1024]{1,0:T(8,128)(2,1)}, u32[]{:S(2)}, u32[]{:S(2)}) collective-permute-start(bf16[128,1024]{1,0:T(8,128)(2,1)} %collective-permute-done.15), channel_id=1, source_target_pairs={{0,64},{1,65},{2,66},{3,67},{4,68},{5,69},{6,70},{7,71},{8,72},{9,... | collective-permute-start | bytes 786440 | tf_op jit(solution)/shard_map/ppermute | solution.py:24
  75.5 3.8 %collective-permute-done.35 = f32[64,256]{1,0:T(8,128)S(1)} collective-permute-done((f32[64,256]{1,0:T(8,128)S(1)}, f32[64,256]{1,0:T(8,128)S(1)}, u32[]{:S(2)}, u32[]{:S(2)}) %collective-permute-start.35) | collective-permute-done | bytes 65568 | tf_op jit(solution)/shard_map/ppermute | solution.py:24
  81.3 2.3 %collective-permute-start.37 = (f32[64,256]{1,0:T(8,128)S(1)}, f32[64,256]{1,0:T(8,128)}, u32[]{:S(2)}, u32[]{:S(2)}) collective-permute-start(f32[64,256]{1,0:T(8,128)S(1)} %add.517), channel_id=1, source_target_pairs={{0,64},{1,65},{2,66},{3,67},{4,68},{5,69},{6,70},{7,71},{8,72},{9,... | collective-permute-start | bytes 196616 | tf_op jit(solution)/shard_map/ppermute | solution.py:24
  83.6 3.2 %collective-permute-start.23 = (bf16[256,1024]{1,0:T(8,128)(2,1)S(1)}, bf16[256,1024]{1,0:T(8,128)(2,1)S(1)}, u32[]{:S(2)}, u32[]{:S(2)}) collective-permute-start(bf16[256,1024]{1,0:T(8,128)(2,1)S(1)} %pad_maximum_fusion.refs_5_), channel_id=1, source_target_pairs={{0,6},{1,7},{2,0},{3,1},{4,2},{5,3},{6,4},{7,5},{8,14},{9,15},{10,... | collective-permute-start | bytes 1572872 | tf_op jit(solution)/shard_map/ppermute | solution.py:24
  90.6 4.9 %collective-permute-done.16 = bf16[128,1024]{1,0:T(8,128)(2,1)S(1)} collective-permute-done((bf16[128,1024]{1,0:T(8,128)(2,1)}, bf16[128,1024]{1,0:T(8,128)(2,1)S(1)}, u32[]{:S(2)}, u32[]{:S(2)}) %collective-permute-start.16) | collective-permute-done | bytes 262176 | tf_op jit(solution)/shard_map/ppermute | solution.py:24
  97.2 4.4 %collective-permute-done.39 = bf16[64,256]{1,0:T(8,128)(2,1)S(1)} collective-permute-done((bf16[64,256]{1,0:T(8,128)(2,1)S(1)}, bf16[64,256]{1,0:T(8,128)(2,1)S(1)}, u32[]{:S(2)}, u32[]{:S(2)}) %collective-permute-start.39) | collective-permute-done | bytes 32800 | tf_op jit(solution)/shard_map/ppermute | solution.py:24
  106.7 2.3 %collective-permute-start.18 = (bf16[256,1024]{1,0:T(8,128)(2,1)S(1)}, bf16[256,1024]{1,0:T(8,128)(2,1)}, u32[]{:S(2)}, u32[]{:S(2)}) collective-permute-start(bf16[256,1024]{1,0:T(8,128)(2,1)S(1)} %constant_dynamic-update-slice_fusion.refs_0_), channel_id=1, source_target_pairs={{0,96},{1,97},{2,98},{3,99},{4,100},{5,101},{6,102},{7,103},{8,104... | collective-permute-start | bytes 1572872 | tf_op jit(solution)/shard_map/ppermute | solution.py:24
  111.3 9.1 %collective-permute-done.18.refs_2_ = bf16[256,1024]{1,0:T(8,128)(2,1)} collective-permute-done((bf16[256,1024]{1,0:T(8,128)(2,1)S(1)}, bf16[256,1024]{1,0:T(8,128)(2,1)}, u32[]{:S(2)}, u32[]{:S(2)}) %collective-permute-start.18) | collective-permute-done | bytes 524320 | tf_op jit(solution)/shard_map/ppermute | solution.py:24
  120.4 3.4 %collective-permute-done.17.refs_1_ = bf16[256,1024]{1,0:T(8,128)(2,1)} collective-permute-done((bf16[256,1024]{1,0:T(8,128)(2,1)S(1)}, bf16[256,1024]{1,0:T(8,128)(2,1)}, u32[]{:S(2)}, u32[]{:S(2)}) %collective-permute-start.17) | collective-permute-done | bytes 524320 | tf_op jit(solution)/shard_map/ppermute | solution.py:24
  128.7 13.0 %shard_map.86 = (f32[2048,1024]{1,0:T(8,128)}, bf16[2048,1024]{1,0:T(8,128)(2,1)}) custom-call(s32[32]{0:T(128)S(1)} %pad_add_fusion.spot, bf16[256,1024]{1,0:T(8,128)(2,1)S(1)} %constant_dynamic-update-slice_fusion.refs_0_, bf16[256,1024]{1,0:T(8,128)(2,1)} %collective-permute-done.17.refs_1_, bf16[256,1024]{1,0:T(8,128)(2,1)} %collective-permute-done.18.refs_2_, ...), custom_call_target="tpu_custom_call" | custom-call | flops 8999999488 | bytes 29360128 | tf_op jit(solution)/shard_map/pallas_call | solution.py:162
  (122 shorter events, 40.8 us)
Async XLA Ops:
  8.6 32.8 %collective-permute-start.9 = (bf16[128,512]{1,0:T(8,128)(2,1)S(1)}, bf16[128,512]{1,0:T(8,128)(2,1)S(1)}, u32[]{:S(2)}, u32[]{:S(2)}) collective-permute-start(bf16[128,512]{1,0:T(8,128)(2,1)S(1)} %get-tuple-element.53), channel_id=1, source_target_pairs={{0,4},{1,5},{2,6},{3,7},{4,0},{5,1},{6,2},{7,3},{8,12},{9,13},{10,... | collective-permute-start | bytes 393224 | tf_op jit(solution)/shard_map/ppermute | solution.py:24
  10.9 29.9 %collective-permute-start.14 = (bf16[128,512]{1,0:T(8,128)(2,1)S(1)}, bf16[128,512]{1,0:T(8,128)(2,1)S(1)}, u32[]{:S(2)}, u32[]{:S(2)}) collective-permute-start(bf16[128,512]{1,0:T(8,128)(2,1)S(1)} %get-tuple-element.54), channel_id=1, source_target_pairs={{0,14},{1,15},{2,8},{3,9},{4,10},{5,11},{6,12},{7,13},{8,6},{9,7},... | collective-permute-start | bytes 393224 | tf_op jit(solution)/shard_map/ppermute | solution.py:24
  15.6 24.7 %collective-permute-start.13 = (bf16[128,512]{1,0:T(8,128)(2,1)S(1)}, bf16[128,512]{1,0:T(8,128)(2,1)S(1)}, u32[]{:S(2)}, u32[]{:S(2)}) collective-permute-start(bf16[128,512]{1,0:T(8,128)(2,1)S(1)} %get-tuple-element.55), channel_id=1, source_target_pairs={{0,12},{1,13},{2,14},{3,15},{4,8},{5,9},{6,10},{7,11},{8,4},{9,5},... | collective-permute-start | bytes 393224 | tf_op jit(solution)/shard_map/ppermute | solution.py:24
  15.6 24.1 %collective-permute-start.12 = (bf16[128,512]{1,0:T(8,128)(2,1)S(1)}, bf16[128,512]{1,0:T(8,128)(2,1)S(1)}, u32[]{:S(2)}, u32[]{:S(2)}) collective-permute-start(bf16[128,512]{1,0:T(8,128)(2,1)S(1)} %get-tuple-element.56), channel_id=1, source_target_pairs={{0,10},{1,11},{2,12},{3,13},{4,14},{5,15},{6,8},{7,9},{8,2},{9,3},... | collective-permute-start | bytes 393224 | tf_op jit(solution)/shard_map/ppermute | solution.py:24
  51.9 16.6 %collective-permute-start.24 = (bf16[128,1024]{1,0:T(8,128)(2,1)S(1)}, bf16[128,1024]{1,0:T(8,128)(2,1)S(1)}, u32[]{:S(2)}, u32[]{:S(2)}) collective-permute-start(bf16[128,1024]{1,0:T(8,128)(2,1)S(1)} %pad_maximum_fusion.1), channel_id=1, source_target_pairs={{0,4},{1,5},{2,6},{3,7},{4,0},{5,1},{6,2},{7,3},{8,12},{9,13},{10,... | collective-permute-start | bytes 786440 | tf_op jit(solution)/shard_map/ppermute | solution.py:24
  55.7 15.2 %collective-permute-start.15 = (bf16[128,1024]{1,0:T(8,128)(2,1)S(1)}, bf16[128,1024]{1,0:T(8,128)(2,1)}, u32[]{:S(2)}, u32[]{:S(2)}) collective-permute-start(bf16[128,1024]{1,0:T(8,128)(2,1)S(1)} %pad_maximum_fusion.1), channel_id=1, source_target_pairs={{0,0},{1,1},{2,32},{3,33},{4,64},{5,65},{6,96},{7,97},{8,16},{9,17... | collective-permute-start | bytes 786440 | tf_op jit(solution)/shard_map/ppermute | solution.py:24
  58.0 14.6 %collective-permute-start.32 = (f32[64,256]{1,0:T(8,128)S(1)}, f32[64,256]{1,0:T(8,128)S(1)}, u32[]{:S(2)}, u32[]{:S(2)}) collective-permute-start(f32[64,256]{1,0:T(8,128)S(1)} %get-tuple-element.60), channel_id=1, source_target_pairs={{0,2},{1,3},{2,4},{3,5},{4,6},{5,7},{6,0},{7,1},{8,10},{9,11},{10,... | collective-permute-start | bytes 196616 | tf_op jit(solution)/shard_map/ppermute | solution.py:24
  61.1 13.9 %collective-permute-start.34 = (f32[64,256]{1,0:T(8,128)S(1)}, f32[64,256]{1,0:T(8,128)S(1)}, u32[]{:S(2)}, u32[]{:S(2)}) collective-permute-start(f32[64,256]{1,0:T(8,128)S(1)} %get-tuple-element.61), channel_id=1, source_target_pairs={{0,6},{1,7},{2,0},{3,1},{4,2},{5,3},{6,4},{7,5},{8,14},{9,15},{10,... | collective-permute-start | bytes 196616 | tf_op jit(solution)/shard_map/ppermute | solution.py:24
  61.1 13.9 %collective-permute-start.33 = (f32[64,256]{1,0:T(8,128)S(1)}, f32[64,256]{1,0:T(8,128)S(1)}, u32[]{:S(2)}, u32[]{:S(2)}) collective-permute-start(f32[64,256]{1,0:T(8,128)S(1)} %get-tuple-element.62), channel_id=1, source_target_pairs={{0,4},{1,5},{2,6},{3,7},{4,0},{5,1},{6,2},{7,3},{8,12},{9,13},{10,... | collective-permute-start | bytes 196616 | tf_op jit(solution)/shard_map/ppermute | solution.py:24
  68.5 15.1 %collective-permute-start.29 = (bf16[128,1024]{1,0:T(8,128)(2,1)S(1)}, bf16[128,1024]{1,0:T(8,128)(2,1)S(1)}, u32[]{:S(2)}, u32[]{:S(2)}) collective-permute-start(bf16[128,1024]{1,0:T(8,128)(2,1)S(1)} %collective-permute-done.24.refs_8_), channel_id=1, source_target_pairs={{0,1},{1,0},{2,3},{3,2},{4,5},{5,4},{6,7},{7,6},{8,9},{9,8},{10,11... | collective-permute-start | bytes 786440 | tf_op jit(solution)/shard_map/ppermute | solution.py:24
  70.9 12.7 %collective-permute-start.25 = (bf16[128,1024]{1,0:T(8,128)(2,1)S(1)}, bf16[128,1024]{1,0:T(8,128)(2,1)}, u32[]{:S(2)}, u32[]{:S(2)}) collective-permute-start(bf16[128,1024]{1,0:T(8,128)(2,1)S(1)} %collective-permute-done.24.refs_8_), channel_id=1, source_target_pairs={{0,8},{1,9},{2,10},{3,11},{4,12},{5,13},{6,14},{7,15},{8,0},{9,1},... | collective-permute-start | bytes 786440 | tf_op jit(solution)/shard_map/ppermute | solution.py:24
  72.7 14.1 %collective-permute-start.19 = (bf16[128,1024]{1,0:T(8,128)(2,1)}, bf16[128,1024]{1,0:T(8,128)(2,1)}, u32[]{:S(2)}, u32[]{:S(2)}) collective-permute-start(bf16[128,1024]{1,0:T(8,128)(2,1)} %collective-permute-done.15), channel_id=1, source_target_pairs={{0,64},{1,65},{2,66},{3,67},{4,68},{5,69},{6,70},{7,71},{8,72},{9,... | collective-permute-start | bytes 786440 | tf_op jit(solution)/shard_map/ppermute | solution.py:24
  79.4 8.2 %collective-permute-start.38 = (f32[64,256]{1,0:T(8,128)S(1)}, f32[64,256]{1,0:T(8,128)S(1)}, u32[]{:S(2)}, u32[]{:S(2)}) collective-permute-start(f32[64,256]{1,0:T(8,128)S(1)} %add.517), channel_id=1, source_target_pairs={{0,96},{1,97},{2,98},{3,99},{4,100},{5,101},{6,102},{7,103},{8,104... | collective-permute-start | bytes 196616 | tf_op jit(solution)/shard_map/ppermute | solution.py:24
  83.6 20.3 %collective-permute-start.23 = (bf16[256,1024]{1,0:T(8,128)(2,1)S(1)}, bf16[256,1024]{1,0:T(8,128)(2,1)S(1)}, u32[]{:S(2)}, u32[]{:S(2)}) collective-permute-start(bf16[256,1024]{1,0:T(8,128)(2,1)S(1)} %pad_maximum_fusion.refs_5_), channel_id=1, source_target_pairs={{0,6},{1,7},{2,0},{3,1},{4,2},{5,3},{6,4},{7,5},{8,14},{9,15},{10,... | collective-permute-start | bytes 1572872 | tf_op jit(solution)/shard_map/ppermute | solution.py:24
  86.8 8.7 %collective-permute-start.16 = (bf16[128,1024]{1,0:T(8,128)(2,1)}, bf16[128,1024]{1,0:T(8,128)(2,1)S(1)}, u32[]{:S(2)}, u32[]{:S(2)}) collective-permute-start(bf16[128,1024]{1,0:T(8,128)(2,1)} %collective-permute-done.15), channel_id=1, source_target_pairs={{0,16},{1,17},{2,18},{3,19},{4,20},{5,21},{6,22},{7,23},{8,24},{9,... | collective-permute-start | bytes 786440 | tf_op jit(solution)/shard_map/ppermute | solution.py:24
  87.6 19.1 %collective-permute-start.22 = (bf16[256,1024]{1,0:T(8,128)(2,1)S(1)}, bf16[256,1024]{1,0:T(8,128)(2,1)S(1)}, u32[]{:S(2)}, u32[]{:S(2)}) collective-permute-start(bf16[256,1024]{1,0:T(8,128)(2,1)S(1)} %pad_maximum_fusion.refs_5_), channel_id=1, source_target_pairs={{0,2},{1,3},{2,4},{3,5},{4,6},{5,7},{6,0},{7,1},{8,10},{9,11},{10,... | collective-permute-start | bytes 1572872 | tf_op jit(solution)/shard_map/ppermute | solution.py:24
  87.9 13.8 %collective-permute-start.30 = (bf16[128,1024]{1,0:T(8,128)(2,1)}, bf16[128,1024]{1,0:T(8,128)(2,1)S(1)}, u32[]{:S(2)}, u32[]{:S(2)}) collective-permute-start(bf16[128,1024]{1,0:T(8,128)(2,1)} %collective-permute-done.25.refs_9_), channel_id=1, source_target_pairs={{0,1},{1,0},{2,3},{3,2},{4,5},{5,4},{6,7},{7,6},{8,9},{9,8},{10,11... | collective-permute-start | bytes 786440 | tf_op jit(solution)/shard_map/ppermute | solution.py:24
  88.0 15.9 %collective-permute-start.20 = (bf16[128,1024]{1,0:T(8,128)(2,1)}, bf16[128,1024]{1,0:T(8,128)(2,1)S(1)}, u32[]{:S(2)}, u32[]{:S(2)}) collective-permute-start(bf16[128,1024]{1,0:T(8,128)(2,1)} %collective-permute-done.19.refs_3_), channel_id=1, source_target_pairs={{0,16},{1,17},{2,18},{3,19},{4,20},{5,21},{6,22},{7,23},{8,24},{9,... | collective-permute-start | bytes 786440 | tf_op jit(solution)/shard_map/ppermute | solution.py:24
  101.6 8.6 %collective-permute-start.26 = (bf16[256,1024]{1,0:T(8,128)(2,1)S(1)}, bf16[256,1024]{1,0:T(8,128)(2,1)S(1)}, u32[]{:S(2)}, u32[]{:S(2)}) collective-permute-start(bf16[256,1024]{1,0:T(8,128)(2,1)S(1)} %pad_maximum_fusion.refs_5_), channel_id=1, source_target_pairs={{0,1},{1,0},{2,3},{3,2},{4,5},{5,4},{6,7},{7,6},{8,9},{9,8},{10,11... | collective-permute-start | bytes 1572872 | tf_op jit(solution)/shard_map/ppermute | solution.py:24
  106.7 13.7 %collective-permute-start.18 = (bf16[256,1024]{1,0:T(8,128)(2,1)S(1)}, bf16[256,1024]{1,0:T(8,128)(2,1)}, u32[]{:S(2)}, u32[]{:S(2)}) collective-permute-start(bf16[256,1024]{1,0:T(8,128)(2,1)S(1)} %constant_dynamic-update-slice_fusion.refs_0_), channel_id=1, source_target_pairs={{0,96},{1,97},{2,98},{3,99},{4,100},{5,101},{6,102},{7,103},{8,104... | collective-permute-start | bytes 1572872 | tf_op jit(solution)/shard_map/ppermute | solution.py:24
  109.0 14.8 %collective-permute-start.17 = (bf16[256,1024]{1,0:T(8,128)(2,1)S(1)}, bf16[256,1024]{1,0:T(8,128)(2,1)}, u32[]{:S(2)}, u32[]{:S(2)}) collective-permute-start(bf16[256,1024]{1,0:T(8,128)(2,1)S(1)} %constant_dynamic-update-slice_fusion.refs_0_), channel_id=1, source_target_pairs={{0,32},{1,33},{2,34},{3,35},{4,36},{5,37},{6,38},{7,39},{8,40},{9,... | collective-permute-start | bytes 1572872 | tf_op jit(solution)/shard_map/ppermute | solution.py:24
  109.7 14.2 %collective-permute-start.28 = (bf16[256,1024]{1,0:T(8,128)(2,1)S(1)}, bf16[256,1024]{1,0:T(8,128)(2,1)}, u32[]{:S(2)}, u32[]{:S(2)}) collective-permute-start(bf16[256,1024]{1,0:T(8,128)(2,1)S(1)} %collective-permute-done.23.refs_7_), channel_id=1, source_target_pairs={{0,1},{1,0},{2,3},{3,2},{4,5},{5,4},{6,7},{7,6},{8,9},{9,8},{10,11... | collective-permute-start | bytes 1572872 | tf_op jit(solution)/shard_map/ppermute | solution.py:24
  109.7 14.2 %collective-permute-start.27 = (bf16[256,1024]{1,0:T(8,128)(2,1)S(1)}, bf16[256,1024]{1,0:T(8,128)(2,1)}, u32[]{:S(2)}, u32[]{:S(2)}) collective-permute-start(bf16[256,1024]{1,0:T(8,128)(2,1)S(1)} %collective-permute-done.22.refs_6_), channel_id=1, source_target_pairs={{0,1},{1,0},{2,3},{3,2},{4,5},{5,4},{6,7},{7,6},{8,9},{9,8},{10,11... | collective-permute-start | bytes 1572872 | tf_op jit(solution)/shard_map/ppermute | solution.py:24
  111.0 12.8 %collective-permute-start.43 = (bf16[256,512]{1,0:T(8,128)(2,1)S(1)}, bf16[256,512]{1,0:T(8,128)(2,1)}, u32[]{:S(2)}, u32[]{:S(2)}) collective-permute-start(bf16[256,512]{1,0:T(8,128)(2,1)S(1)} %pad_maximum_fusion.2.refs_15_), channel_id=1, source_target_pairs={{0,1},{1,0},{2,3},{3,2},{4,5},{5,4},{6,7},{7,6},{8,9},{9,8},{10,11... | collective-permute-start | bytes 786440 | tf_op jit(solution)/shard_map/ppermute | solution.py:24
  (28 other events, 216.0 us)

commit v3 on v1

--- a/solution.py
+++ b/solution.py
@@ -57,10 +57,6 @@
     return lax.dynamic_slice_in_dim(value, start, count, 0)
 
 
-def put(buffer, piece, start):
-    return lax.dynamic_update_slice_in_dim(buffer, piece, start, 0)
-
-
 def joined(mine, theirs, mine_second, axis):
     return jnp.where(
         mine_second == 1,
@@ -69,6 +65,10 @@
     )
 
 
+def put(buffer, piece, start):
+    return lax.dynamic_update_slice_in_dim(buffer, piece, start, 0)
+
+
 def mm(a, b):
     return jnp.dot(a, b, preferred_element_type=F32)
 
@@ -94,16 +94,10 @@
     piece_sem, fixed_sem, load_sem, save_sem, panel_sem = refs[28:]
 
     def fetch(i):
-        if i >= 24:
-            source, target, height = pieces[15 + i - 24], gram_here, 256
-        else:
-            group, half = i // 8, i % 8
-            source = pieces[group * 5 + (half // 2 if half < 6 else half - 3)]
-            if half < 6:
-                source = source.at[pl.ds(half % 2 * 128, 128)]
-            target, height = cols if group == 0 else block, 128
+        height = pieces[i].shape[0]
         at = pl.ds(pl.multiple_of(spot[i] * 128, 128), height)
-        return pltpu.make_async_copy(source, target.at[at], piece_sem.at[i])
+        target = cols if i < 5 else block if i < 15 else gram_here
+        return pltpu.make_async_copy(pieces[i], target.at[at], piece_sem.at[i])
 
     def rows_of(i):
         return pl.ds(pl.multiple_of(i * SLAB, SLAB), SLAB)
@@ -123,10 +117,10 @@
 
     constants = pltpu.make_async_copy(inverses.at[1], inverse_here, fixed_sem)
     constants.start()
-    early = (*range(8), 24, 25)
+    early = (0, 1, 2, 3, 4, 15, 16)
     for i in early:
         fetch(i).start()
-    for i in range(8, 24):
+    for i in range(5, 15):
         fetch(i).start()
     for i in range(SLABS):
         load(i).start()
@@ -137,7 +131,7 @@
     second = second_panel(cols, inverse_here, gram_here, sign[...])
     strip[:, :512] = cols[:, :512] * sign[:, :512]
     strip[:, 512:] = second * sign[:, 512:]
-    for i in range(8, 24):
+    for i in range(5, 15):
         fetch(i).wait()
 
     def step(i, carry):
@@ -177,7 +171,7 @@
                 pltpu.VMEM((2048, 1024), F32),
                 pltpu.VMEM((512, 512), BF),
                 pltpu.VMEM((512, 512), BF),
-                pltpu.SemaphoreType.DMA((26,)),
+                pltpu.SemaphoreType.DMA((17,)),
                 pltpu.SemaphoreType.DMA,
                 pltpu.SemaphoreType.DMA((SLABS,)),
                 pltpu.SemaphoreType.DMA((SLABS,)),
@@ -237,14 +231,16 @@
         picked,
     )
     cols = (picked * rescale[None, :]).astype(BF)
-    cols = jnp.concatenate([mm(cols[:, :512], inverses[0]).astype(BF), cols[:, 512:]], axis=1)
-
-    pair = jnp.concatenate([cols, move(cols, other_zh)], axis=0)
+    cols = cols.at[:, :512].set(mm(cols[:, :512], inverses[0]).astype(BF))
+
+    pair = put(jnp.zeros((256, 1024), BF), cols, zh * 128)
+    pair = put(pair, move(cols, other_zh), (1 - zh) * 128)
 
     first = zh * 2 + y // 2
     part = zl ^ (y % 2) ^ zh
     piece = move(cols, to_strip)
-    strip = jnp.concatenate([piece, move(piece, other_zl)], axis=0)
+    strip = put(jnp.zeros((256, 1024), BF), piece, part * 128)
+    strip = put(strip, move(piece, other_zl), (1 - part) * 128)
     strips = [strip] + [move(strip, along_x(step)) for step in (1, 3)]
     across = move(piece, along_x(2))
     strips += [across, move(across, other_zl)]
@@ -265,17 +261,17 @@
     one, two, three = [move(total, flip_x(bit)) for bit in (1, 2, 3)]
     total = (total + one) + (two + three)
     low = total.astype(BF)
-    low = joined(low, move(low, other_zh), zh, 1)
-    whole = put(jnp.zeros((256, 512), BF), low, y * 64)
+    low2 = joined(low, move(low, other_zh), zh, 1)
+    low3 = put(jnp.zeros((256, 512), BF), low2, y * 64)
     for step in (1, 2, 3):
-        whole = put(whole, move(low, along_y(step)), ((y - step) % 4) * 64)
-    low = whole
-    grams = [low, move(low, other_core)]
-
-    index = lax.iota(jnp.int32, 24)
-    kind, index = index // 8, index % 8
-    hop = jnp.where(index < 6, (index // 2 * (index // 2 + 1)) // 2, 2)
-    lower = jnp.where(kind == 0, part, zh) ^ (index % 2)
+        low3 = put(low3, move(low2, along_y(step)), ((y - step) % 4) * 64)
+    grams = [low3, move(low3, other_core)]
+
+    index = lax.iota(jnp.int32, 15)
+    kind, index = index // 5, index % 5
+    hop = jnp.where(index < 3, (index * index + index) // 2, 2)
+    half = jnp.where(kind == 0, part, zh)
+    lower = jnp.where(index == 3, half, jnp.where(index == 4, 1 - half, 0))
     base = jnp.where(kind == 0, x - first, y)
     spot = (base - hop) % 4 * 2 + lower
     spot += jnp.where(kind == 0, 0, jnp.where(kind == 1, k, 1 - k)) * 8

time: 138 us -> 139 us (level)
  transfers between devices with their start and end apart: 37 -> 37, of which waited for: 13 -> 12; matrix products, arithmetic and copies ran while one was open for 5% -> 6% of each run, Pallas kernels for 0% -> 0%
where the time goes in v3:
time: 139 us; the launch traced here: 138 us
  starting transfers between devices  55.6 us (40%)
  waiting for transfers between devices  52.8 us (38%)
  Pallas kernels  12 us (9%)
  matrix products  8.28 us (6%)
  other arithmetic  4.03 us (3%)
  between operations  2.32 us (2%)
  local copies, waits for them, and re-layouts  2.25 us (2%)
    ppermute x37, starting transfers between devices, move(): return lax.ppermute(value, ('row', 'col'), pairs)  55.6 us
    ppermute x37, waiting for transfers between devices, move(): return lax.ppermute(value, ('row', 'col'), pairs)  52.8 us
    pallas_call x1, Pallas kernels, tail(): pl.pallas_call(tail_kernel, grid_spec=pltpu.PrefetchScalarGridSpec(num_sc...  12 us
    dot_general x11, matrix products, mm(): return jnp.dot(a, b, preferred_element_type=F32)  8.01 us
  transfers between devices with their start and end apart: 37, of which 12 were waited for; matrix products, arithmetic and copies ran while one was open for 6% of the time, Pallas kernels for 0%

profile of v3, /device:TPU:8, one launch (start us, length us, event | category | flops | bytes accessed | tf_op | source)
XLA Modules:
  0.0 137.5 jit_solution(10649127127993954968)
XLA Ops:
  9.2 2.4 %collective-permute-start.9 = (bf16[128,512]{1,0:T(8,128)(2,1)S(1)}, bf16[128,512]{1,0:T(8,128)(2,1)S(1)}, u32[]{:S(2)}, u32[]{:S(2)}) collective-permute-start(bf16[128,512]{1,0:T(8,128)(2,1)S(1)} %get-tuple-element.67), channel_id=1, source_target_pairs={{0,4},{1,5},{2,6},{3,7},{4,0},{5,1},{6,2},{7,3},{8,12},{9,13},{10,... | collective-permute-start | bytes 393224 | tf_op jit(solution)/shard_map/ppermute | solution.py:24
  11.6 4.7 %collective-permute-start.14 = (bf16[128,512]{1,0:T(8,128)(2,1)S(1)}, bf16[128,512]{1,0:T(8,128)(2,1)S(1)}, u32[]{:S(2)}, u32[]{:S(2)}) collective-permute-start(bf16[128,512]{1,0:T(8,128)(2,1)S(1)} %get-tuple-element.68), channel_id=1, source_target_pairs={{0,14},{1,15},{2,8},{3,9},{4,10},{5,11},{6,12},{7,13},{8,6},{9,7},... | collective-permute-start | bytes 393224 | tf_op jit(solution)/shard_map/ppermute | solution.py:24
  16.2 4.9 %collective-permute-start.12 = (bf16[128,512]{1,0:T(8,128)(2,1)S(1)}, bf16[128,512]{1,0:T(8,128)(2,1)S(1)}, u32[]{:S(2)}, u32[]{:S(2)}) collective-permute-start(bf16[128,512]{1,0:T(8,128)(2,1)S(1)} %get-tuple-element.70), channel_id=1, source_target_pairs={{0,10},{1,11},{2,12},{3,13},{4,14},{5,15},{6,8},{7,9},{8,2},{9,3},... | collective-permute-start | bytes 393224 | tf_op jit(solution)/shard_map/ppermute | solution.py:24
  23.3 5.0 %collective-permute-done.8 = bf16[128,512]{1,0:T(8,128)(2,1)S(1)} collective-permute-done((bf16[128,512]{1,0:T(8,128)(2,1)S(1)}, bf16[128,512]{1,0:T(8,128)(2,1)S(1)}, u32[]{:S(2)}, u32[]{:S(2)}) %collective-permute-start.8) | collective-permute-done | bytes 131104 | tf_op jit(solution)/shard_map/ppermute | solution.py:24
  28.3 2.0 %collective-permute-start.10 = (bf16[128,512]{1,0:T(8,128)(2,1)S(1)}, bf16[128,512]{1,0:T(8,128)(2,1)S(1)}, u32[]{:S(2)}, u32[]{:S(2)}) collective-permute-start(bf16[128,512]{1,0:T(8,128)(2,1)S(1)} %get-tuple-element.72), channel_id=1, source_target_pairs={{0,6},{1,7},{2,0},{3,1},{4,2},{5,3},{6,4},{7,5},{8,14},{9,15},{10,... | collective-permute-start | bytes 393224 | tf_op jit(solution)/shard_map/ppermute | solution.py:24
  30.9 2.4 %collective-permute-done.10 = bf16[128,512]{1,0:T(8,128)(2,1)S(1)} collective-permute-done((bf16[128,512]{1,0:T(8,128)(2,1)S(1)}, bf16[128,512]{1,0:T(8,128)(2,1)S(1)}, u32[]{:S(2)}, u32[]{:S(2)}) %collective-permute-start.10) | collective-permute-done | bytes 131104 | tf_op jit(solution)/shard_map/ppermute | solution.py:24
  33.3 3.2 %collective-permute-start.11 = (bf16[128,512]{1,0:T(8,128)(2,1)S(1)}, bf16[128,512]{1,0:T(8,128)(2,1)S(1)}, u32[]{:S(2)}, u32[]{:S(2)}) collective-permute-start(bf16[128,512]{1,0:T(8,128)(2,1)S(1)} %get-tuple-element.71), channel_id=1, source_target_pairs={{0,8},{1,9},{2,10},{3,11},{4,12},{5,13},{6,14},{7,15},{8,0},{9,1},... | collective-permute-start | bytes 393224 | tf_op jit(solution)/shard_map/ppermute | solution.py:24
  37.0 2.8 %collective-permute-done.11 = bf16[128,512]{1,0:T(8,128)(2,1)S(1)} collective-permute-done((bf16[128,512]{1,0:T(8,128)(2,1)S(1)}, bf16[128,512]{1,0:T(8,128)(2,1)S(1)}, u32[]{:S(2)}, u32[]{:S(2)}) %collective-permute-start.11) | collective-permute-done | bytes 131104 | tf_op jit(solution)/shard_map/ppermute | solution.py:24
  44.7 3.2 %collective-permute-start.21 = (bf16[128,1024]{1,0:T(8,128)(2,1)S(1)}, bf16[128,1024]{1,0:T(8,128)(2,1)S(1)}, u32[]{:S(2)}, u32[]{:S(2)}) collective-permute-start(bf16[128,1024]{1,0:T(8,128)(2,1)S(1)} %fusion.46), channel_id=1, source_target_pairs={{0,8},{1,9},{2,10},{3,11},{4,12},{5,13},{6,14},{7,15},{8,0},{9,1},... | collective-permute-start | bytes 786440 | tf_op jit(solution)/shard_map/ppermute | solution.py:24
  48.0 4.6 %collective-permute-done.21 = bf16[128,1024]{1,0:T(8,128)(2,1)S(1)} collective-permute-done((bf16[128,1024]{1,0:T(8,128)(2,1)S(1)}, bf16[128,1024]{1,0:T(8,128)(2,1)S(1)}, u32[]{:S(2)}, u32[]{:S(2)}) %collective-permute-start.21) | collective-permute-done | bytes 262176 | tf_op jit(solution)/shard_map/ppermute | solution.py:24
  53.1 3.8 %collective-permute-start.24 = (bf16[128,1024]{1,0:T(8,128)(2,1)S(1)}, bf16[128,1024]{1,0:T(8,128)(2,1)S(1)}, u32[]{:S(2)}, u32[]{:S(2)}) collective-permute-start(bf16[128,1024]{1,0:T(8,128)(2,1)S(1)} %fusion.46), channel_id=1, source_target_pairs={{0,4},{1,5},{2,6},{3,7},{4,0},{5,1},{6,2},{7,3},{8,12},{9,13},{10,... | collective-permute-start | bytes 786440 | tf_op jit(solution)/shard_map/ppermute | solution.py:24
  57.1 2.0 %collective-permute-start.34 = (f32[64,256]{1,0:T(8,128)S(1)}, f32[64,256]{1,0:T(8,128)S(1)}, u32[]{:S(2)}, u32[]{:S(2)}) collective-permute-start(f32[64,256]{1,0:T(8,128)S(1)} %get-tuple-element.75), channel_id=1, source_target_pairs={{0,6},{1,7},{2,0},{3,1},{4,2},{5,3},{6,4},{7,5},{8,14},{9,15},{10,... | collective-permute-start | bytes 196616 | tf_op jit(solution)/shard_map/ppermute | solution.py:24
  60.5 3.6 %collective-permute-start.15 = (bf16[128,1024]{1,0:T(8,128)(2,1)S(1)}, bf16[128,1024]{1,0:T(8,128)(2,1)S(1)}, u32[]{:S(2)}, u32[]{:S(2)}) collective-permute-start(bf16[128,1024]{1,0:T(8,128)(2,1)S(1)} %fusion.46), channel_id=1, source_target_pairs={{0,0},{1,1},{2,32},{3,33},{4,64},{5,65},{6,96},{7,97},{8,16},{9,17... | collective-permute-start | bytes 786440 | tf_op jit(solution)/shard_map/ppermute | solution.py:24
  64.9 2.2 %collective-permute-start.25 = (bf16[128,1024]{1,0:T(8,128)(2,1)S(1)}, bf16[128,1024]{1,0:T(8,128)(2,1)S(1)}, u32[]{:S(2)}, u32[]{:S(2)}) collective-permute-start(bf16[128,1024]{1,0:T(8,128)(2,1)S(1)} %collective-permute-done.24.refs_8_), channel_id=1, source_target_pairs={{0,8},{1,9},{2,10},{3,11},{4,12},{5,13},{6,14},{7,15},{8,0},{9,1},... | collective-permute-start | bytes 786440 | tf_op jit(solution)/shard_map/ppermute | solution.py:24
  67.1 5.2 %collective-permute-done.33 = f32[64,256]{1,0:T(8,128)S(1)} collective-permute-done((f32[64,256]{1,0:T(8,128)S(1)}, f32[64,256]{1,0:T(8,128)S(1)}, u32[]{:S(2)}, u32[]{:S(2)}) %collective-permute-start.33) | collective-permute-done | bytes 65568 | tf_op jit(solution)/shard_map/ppermute | solution.py:24
  72.4 7.2 %collective-permute-done.15 = bf16[128,1024]{1,0:T(8,128)(2,1)S(1)} collective-permute-done((bf16[128,1024]{1,0:T(8,128)(2,1)S(1)}, bf16[128,1024]{1,0:T(8,128)(2,1)S(1)}, u32[]{:S(2)}, u32[]{:S(2)}) %collective-permute-start.15) | collective-permute-done | bytes 262176 | tf_op jit(solution)/shard_map/ppermute | solution.py:24
  82.0 2.9 %collective-permute-start.37 = (f32[64,256]{1,0:T(8,128)S(1)}, f32[64,256]{1,0:T(8,128)S(1)}, u32[]{:S(2)}, u32[]{:S(2)}) collective-permute-start(f32[64,256]{1,0:T(8,128)S(1)} %add.533), channel_id=1, source_target_pairs={{0,64},{1,65},{2,66},{3,67},{4,68},{5,69},{6,70},{7,71},{8,72},{9,... | collective-permute-start | bytes 196616 | tf_op jit(solution)/shard_map/ppermute | solution.py:24
  85.0 5.5 %collective-permute-done.38 = f32[64,256]{1,0:T(8,128)S(1)} collective-permute-done((f32[64,256]{1,0:T(8,128)S(1)}, f32[64,256]{1,0:T(8,128)S(1)}, u32[]{:S(2)}, u32[]{:S(2)}) %collective-permute-start.38) | collective-permute-done | bytes 65568 | tf_op jit(solution)/shard_map/ppermute | solution.py:24
  90.5 2.0 %collective-permute-start.22 = (bf16[256,1024]{1,0:T(8,128)(2,1)S(1)}, bf16[256,1024]{1,0:T(8,128)(2,1)S(1)}, u32[]{:S(2)}, u32[]{:S(2)}) collective-permute-start(bf16[256,1024]{1,0:T(8,128)(2,1)S(1)} %constant_dynamic-update-slice_fusion.4.refs_5_), channel_id=1, source_target_pairs={{0,2},{1,3},{2,4},{3,5},{4,6},{5,7},{6,0},{7,1},{8,10},{9,11},{10,... | collective-permute-start | bytes 1572872 | tf_op jit(solution)/shard_map/ppermute | solution.py:24
  94.0 7.3 %collective-permute-done.39 = bf16[64,256]{1,0:T(8,128)(2,1)S(1)} collective-permute-done((bf16[64,256]{1,0:T(8,128)(2,1)S(1)}, bf16[64,256]{1,0:T(8,128)(2,1)S(1)}, u32[]{:S(2)}, u32[]{:S(2)}) %collective-permute-start.39) | collective-permute-done | bytes 32800 | tf_op jit(solution)/shard_map/ppermute | solution.py:24
  102.9 2.7 %collective-permute-start.41 = (bf16[64,512]{1,0:T(8,128)(2,1)S(1)}, bf16[64,512]{1,0:T(8,128)(2,1)S(1)}, u32[]{:S(2)}, u32[]{:S(2)}) collective-permute-start(bf16[64,512]{1,0:T(8,128)(2,1)S(1)} %get-tuple-element.43), channel_id=1, source_target_pairs={{0,4},{1,5},{2,6},{3,7},{4,0},{5,1},{6,2},{7,3},{8,12},{9,13},{10,... | collective-permute-start | bytes 196616 | tf_op jit(solution)/shard_map/ppermute | solution.py:24
  106.2 4.4 %collective-permute-start.42 = (bf16[64,512]{1,0:T(8,128)(2,1)S(1)}, bf16[64,512]{1,0:T(8,128)(2,1)S(1)}, u32[]{:S(2)}, u32[]{:S(2)}) collective-permute-start(bf16[64,512]{1,0:T(8,128)(2,1)S(1)} %get-tuple-element.43), channel_id=1, source_target_pairs={{0,6},{1,7},{2,0},{3,1},{4,2},{5,3},{6,4},{7,5},{8,14},{9,15},{10,... | collective-permute-start | bytes 196616 | tf_op jit(solution)/shard_map/ppermute | solution.py:24
  113.9 10.0 %collective-permute-done.18.refs_2_ = bf16[256,1024]{1,0:T(8,128)(2,1)S(1)} collective-permute-done((bf16[256,1024]{1,0:T(8,128)(2,1)S(1)}, bf16[256,1024]{1,0:T(8,128)(2,1)S(1)}, u32[]{:S(2)}, u32[]{:S(2)}) %collective-permute-start.18) | collective-permute-done | bytes 524320 | tf_op jit(solution)/shard_map/ppermute | solution.py:24
  125.3 12.0 %shard_map.86 = (f32[2048,1024]{1,0:T(8,128)}, bf16[2048,1024]{1,0:T(8,128)(2,1)}) custom-call(s32[17]{0:T(128)S(1)} %pad_add_fusion.spot, bf16[256,1024]{1,0:T(8,128)(2,1)S(1)} %constant_dynamic-update-slice_fusion.6.refs_0_, bf16[256,1024]{1,0:T(8,128)(2,1)S(1)} %collective-permute-done.17.refs_1_, bf16[256,1024]{1,0:T(8,128)(2,1)S(1)} %collective-permute-done.18.refs_2_, ...), custom_call_target="tpu_custom_call" | custom-call | flops 8999999488 | bytes 29360128 | tf_op jit(solution)/shard_map/pallas_call | solution.py:159
  (106 shorter events, 29.3 us)
Async XLA Ops:
  9.2 32.8 %collective-permute-start.9 = (bf16[128,512]{1,0:T(8,128)(2,1)S(1)}, bf16[128,512]{1,0:T(8,128)(2,1)S(1)}, u32[]{:S(2)}, u32[]{:S(2)}) collective-permute-start(bf16[128,512]{1,0:T(8,128)(2,1)S(1)} %get-tuple-element.67), channel_id=1, source_target_pairs={{0,4},{1,5},{2,6},{3,7},{4,0},{5,1},{6,2},{7,3},{8,12},{9,13},{10,... | collective-permute-start | bytes 393224 | tf_op jit(solution)/shard_map/ppermute | solution.py:24
  11.6 29.9 %collective-permute-start.14 = (bf16[128,512]{1,0:T(8,128)(2,1)S(1)}, bf16[128,512]{1,0:T(8,128)(2,1)S(1)}, u32[]{:S(2)}, u32[]{:S(2)}) collective-permute-start(bf16[128,512]{1,0:T(8,128)(2,1)S(1)} %get-tuple-element.68), channel_id=1, source_target_pairs={{0,14},{1,15},{2,8},{3,9},{4,10},{5,11},{6,12},{7,13},{8,6},{9,7},... | collective-permute-start | bytes 393224 | tf_op jit(solution)/shard_map/ppermute | solution.py:24
  16.2 24.6 %collective-permute-start.13 = (bf16[128,512]{1,0:T(8,128)(2,1)S(1)}, bf16[128,512]{1,0:T(8,128)(2,1)S(1)}, u32[]{:S(2)}, u32[]{:S(2)}) collective-permute-start(bf16[128,512]{1,0:T(8,128)(2,1)S(1)} %get-tuple-element.69), channel_id=1, source_target_pairs={{0,12},{1,13},{2,14},{3,15},{4,8},{5,9},{6,10},{7,11},{8,4},{9,5},... | collective-permute-start | bytes 393224 | tf_op jit(solution)/shard_map/ppermute | solution.py:24
  16.2 24.1 %collective-permute-start.12 = (bf16[128,512]{1,0:T(8,128)(2,1)S(1)}, bf16[128,512]{1,0:T(8,128)(2,1)S(1)}, u32[]{:S(2)}, u32[]{:S(2)}) collective-permute-start(bf16[128,512]{1,0:T(8,128)(2,1)S(1)} %get-tuple-element.70), channel_id=1, source_target_pairs={{0,10},{1,11},{2,12},{3,13},{4,14},{5,15},{6,8},{7,9},{8,2},{9,3},... | collective-permute-start | bytes 393224 | tf_op jit(solution)/shard_map/ppermute | solution.py:24
  53.1 11.0 %collective-permute-start.24 = (bf16[128,1024]{1,0:T(8,128)(2,1)S(1)}, bf16[128,1024]{1,0:T(8,128)(2,1)S(1)}, u32[]{:S(2)}, u32[]{:S(2)}) collective-permute-start(bf16[128,1024]{1,0:T(8,128)(2,1)S(1)} %fusion.46), channel_id=1, source_target_pairs={{0,4},{1,5},{2,6},{3,7},{4,0},{5,1},{6,2},{7,3},{8,12},{9,13},{10,... | collective-permute-start | bytes 786440 | tf_op jit(solution)/shard_map/ppermute | solution.py:24
  57.1 10.0 %collective-permute-start.34 = (f32[64,256]{1,0:T(8,128)S(1)}, f32[64,256]{1,0:T(8,128)S(1)}, u32[]{:S(2)}, u32[]{:S(2)}) collective-permute-start(f32[64,256]{1,0:T(8,128)S(1)} %get-tuple-element.75), channel_id=1, source_target_pairs={{0,6},{1,7},{2,0},{3,1},{4,2},{5,3},{6,4},{7,5},{8,14},{9,15},{10,... | collective-permute-start | bytes 196616 | tf_op jit(solution)/shard_map/ppermute | solution.py:24
  59.1 13.2 %collective-permute-start.33 = (f32[64,256]{1,0:T(8,128)S(1)}, f32[64,256]{1,0:T(8,128)S(1)}, u32[]{:S(2)}, u32[]{:S(2)}) collective-permute-start(f32[64,256]{1,0:T(8,128)S(1)} %get-tuple-element.76), channel_id=1, source_target_pairs={{0,4},{1,5},{2,6},{3,7},{4,0},{5,1},{6,2},{7,3},{8,12},{9,13},{10,... | collective-permute-start | bytes 196616 | tf_op jit(solution)/shard_map/ppermute | solution.py:24
  60.5 19.0 %collective-permute-start.15 = (bf16[128,1024]{1,0:T(8,128)(2,1)S(1)}, bf16[128,1024]{1,0:T(8,128)(2,1)S(1)}, u32[]{:S(2)}, u32[]{:S(2)}) collective-permute-start(bf16[128,1024]{1,0:T(8,128)(2,1)S(1)} %fusion.46), channel_id=1, source_target_pairs={{0,0},{1,1},{2,32},{3,33},{4,64},{5,65},{6,96},{7,97},{8,16},{9,17... | collective-permute-start | bytes 786440 | tf_op jit(solution)/shard_map/ppermute | solution.py:24
  64.1 17.9 %collective-permute-start.29 = (bf16[128,1024]{1,0:T(8,128)(2,1)S(1)}, bf16[128,1024]{1,0:T(8,128)(2,1)S(1)}, u32[]{:S(2)}, u32[]{:S(2)}) collective-permute-start(bf16[128,1024]{1,0:T(8,128)(2,1)S(1)} %collective-permute-done.24.refs_8_), channel_id=1, source_target_pairs={{0,1},{1,0},{2,3},{3,2},{4,5},{5,4},{6,7},{7,6},{8,9},{9,8},{10,11... | collective-permute-start | bytes 786440 | tf_op jit(solution)/shard_map/ppermute | solution.py:24
  64.9 20.0 %collective-permute-start.25 = (bf16[128,1024]{1,0:T(8,128)(2,1)S(1)}, bf16[128,1024]{1,0:T(8,128)(2,1)S(1)}, u32[]{:S(2)}, u32[]{:S(2)}) collective-permute-start(bf16[128,1024]{1,0:T(8,128)(2,1)S(1)} %collective-permute-done.24.refs_8_), channel_id=1, source_target_pairs={{0,8},{1,9},{2,10},{3,11},{4,12},{5,13},{6,14},{7,15},{8,0},{9,1},... | collective-permute-start | bytes 786440 | tf_op jit(solution)/shard_map/ppermute | solution.py:24
  79.5 13.0 %collective-permute-start.19 = (bf16[128,1024]{1,0:T(8,128)(2,1)S(1)}, bf16[128,1024]{1,0:T(8,128)(2,1)S(1)}, u32[]{:S(2)}, u32[]{:S(2)}) collective-permute-start(bf16[128,1024]{1,0:T(8,128)(2,1)S(1)} %collective-permute-done.15), channel_id=1, source_target_pairs={{0,64},{1,65},{2,66},{3,67},{4,68},{5,69},{6,70},{7,71},{8,72},{9,... | collective-permute-start | bytes 786440 | tf_op jit(solution)/shard_map/ppermute | solution.py:24
  80.5 12.2 %collective-permute-start.16 = (bf16[128,1024]{1,0:T(8,128)(2,1)S(1)}, bf16[128,1024]{1,0:T(8,128)(2,1)S(1)}, u32[]{:S(2)}, u32[]{:S(2)}) collective-permute-start(bf16[128,1024]{1,0:T(8,128)(2,1)S(1)} %collective-permute-done.15), channel_id=1, source_target_pairs={{0,16},{1,17},{2,18},{3,19},{4,20},{5,21},{6,22},{7,23},{8,24},{9,... | collective-permute-start | bytes 786440 | tf_op jit(solution)/shard_map/ppermute | solution.py:24
  80.5 10.0 %collective-permute-start.38 = (f32[64,256]{1,0:T(8,128)S(1)}, f32[64,256]{1,0:T(8,128)S(1)}, u32[]{:S(2)}, u32[]{:S(2)}) collective-permute-start(f32[64,256]{1,0:T(8,128)S(1)} %add.533), channel_id=1, source_target_pairs={{0,96},{1,97},{2,98},{3,99},{4,100},{5,101},{6,102},{7,103},{8,104... | collective-permute-start | bytes 196616 | tf_op jit(solution)/shard_map/ppermute | solution.py:24
  90.5 20.1 %collective-permute-start.23 = (bf16[256,1024]{1,0:T(8,128)(2,1)S(1)}, bf16[256,1024]{1,0:T(8,128)(2,1)S(1)}, u32[]{:S(2)}, u32[]{:S(2)}) collective-permute-start(bf16[256,1024]{1,0:T(8,128)(2,1)S(1)} %constant_dynamic-update-slice_fusion.4.refs_5_), channel_id=1, source_target_pairs={{0,6},{1,7},{2,0},{3,1},{4,2},{5,3},{6,4},{7,5},{8,14},{9,15},{10,... | collective-permute-start | bytes 1572872 | tf_op jit(solution)/shard_map/ppermute | solution.py:24
  90.5 20.4 %collective-permute-start.22 = (bf16[256,1024]{1,0:T(8,128)(2,1)S(1)}, bf16[256,1024]{1,0:T(8,128)(2,1)S(1)}, u32[]{:S(2)}, u32[]{:S(2)}) collective-permute-start(bf16[256,1024]{1,0:T(8,128)(2,1)S(1)} %constant_dynamic-update-slice_fusion.4.refs_5_), channel_id=1, source_target_pairs={{0,2},{1,3},{2,4},{3,5},{4,6},{5,7},{6,0},{7,1},{8,10},{9,11},{10,... | collective-permute-start | bytes 1572872 | tf_op jit(solution)/shard_map/ppermute | solution.py:24
  92.6 8.8 %collective-permute-start.30 = (bf16[128,1024]{1,0:T(8,128)(2,1)S(1)}, bf16[128,1024]{1,0:T(8,128)(2,1)S(1)}, u32[]{:S(2)}, u32[]{:S(2)}) collective-permute-start(bf16[128,1024]{1,0:T(8,128)(2,1)S(1)} %collective-permute-done.25.refs_9_), channel_id=1, source_target_pairs={{0,1},{1,0},{2,3},{3,2},{4,5},{5,4},{6,7},{7,6},{8,9},{9,8},{10,11... | collective-permute-start | bytes 786440 | tf_op jit(solution)/shard_map/ppermute | solution.py:24
  92.6 10.3 %collective-permute-start.20 = (bf16[128,1024]{1,0:T(8,128)(2,1)S(1)}, bf16[128,1024]{1,0:T(8,128)(2,1)S(1)}, u32[]{:S(2)}, u32[]{:S(2)}) collective-permute-start(bf16[128,1024]{1,0:T(8,128)(2,1)S(1)} %collective-permute-done.19.refs_3_), channel_id=1, source_target_pairs={{0,16},{1,17},{2,18},{3,19},{4,20},{5,21},{6,22},{7,23},{8,24},{9,... | collective-permute-start | bytes 786440 | tf_op jit(solution)/shard_map/ppermute | solution.py:24
  101.3 11.9 %collective-permute-start.26 = (bf16[256,1024]{1,0:T(8,128)(2,1)S(1)}, bf16[256,1024]{1,0:T(8,128)(2,1)S(1)}, u32[]{:S(2)}, u32[]{:S(2)}) collective-permute-start(bf16[256,1024]{1,0:T(8,128)(2,1)S(1)} %constant_dynamic-update-slice_fusion.4.refs_5_), channel_id=1, source_target_pairs={{0,1},{1,0},{2,3},{3,2},{4,5},{5,4},{6,7},{7,6},{8,9},{9,8},{10,11... | collective-permute-start | bytes 1572872 | tf_op jit(solution)/shard_map/ppermute | solution.py:24
  102.9 9.8 %collective-permute-start.41 = (bf16[64,512]{1,0:T(8,128)(2,1)S(1)}, bf16[64,512]{1,0:T(8,128)(2,1)S(1)}, u32[]{:S(2)}, u32[]{:S(2)}) collective-permute-start(bf16[64,512]{1,0:T(8,128)(2,1)S(1)} %get-tuple-element.43), channel_id=1, source_target_pairs={{0,4},{1,5},{2,6},{3,7},{4,0},{5,1},{6,2},{7,3},{8,12},{9,13},{10,... | collective-permute-start | bytes 196616 | tf_op jit(solution)/shard_map/ppermute | solution.py:24
  110.6 13.3 %collective-permute-start.18 = (bf16[256,1024]{1,0:T(8,128)(2,1)S(1)}, bf16[256,1024]{1,0:T(8,128)(2,1)S(1)}, u32[]{:S(2)}, u32[]{:S(2)}) collective-permute-start(bf16[256,1024]{1,0:T(8,128)(2,1)S(1)} %constant_dynamic-update-slice_fusion.6.refs_0_), channel_id=1, source_target_pairs={{0,96},{1,97},{2,98},{3,99},{4,100},{5,101},{6,102},{7,103},{8,104... | collective-permute-start | bytes 1572872 | tf_op jit(solution)/shard_map/ppermute | solution.py:24
  111.0 14.4 %collective-permute-start.17 = (bf16[256,1024]{1,0:T(8,128)(2,1)S(1)}, bf16[256,1024]{1,0:T(8,128)(2,1)S(1)}, u32[]{:S(2)}, u32[]{:S(2)}) collective-permute-start(bf16[256,1024]{1,0:T(8,128)(2,1)S(1)} %constant_dynamic-update-slice_fusion.6.refs_0_), channel_id=1, source_target_pairs={{0,32},{1,33},{2,34},{3,35},{4,36},{5,37},{6,38},{7,39},{8,40},{9,... | collective-permute-start | bytes 1572872 | tf_op jit(solution)/shard_map/ppermute | solution.py:24
  112.7 12.6 %collective-permute-start.28 = (bf16[256,1024]{1,0:T(8,128)(2,1)S(1)}, bf16[256,1024]{1,0:T(8,128)(2,1)S(1)}, u32[]{:S(2)}, u32[]{:S(2)}) collective-permute-start(bf16[256,1024]{1,0:T(8,128)(2,1)S(1)} %collective-permute-done.23.refs_7_), channel_id=1, source_target_pairs={{0,1},{1,0},{2,3},{3,2},{4,5},{5,4},{6,7},{7,6},{8,9},{9,8},{10,11... | collective-permute-start | bytes 1572872 | tf_op jit(solution)/shard_map/ppermute | solution.py:24
  112.7 12.6 %collective-permute-start.27 = (bf16[256,1024]{1,0:T(8,128)(2,1)S(1)}, bf16[256,1024]{1,0:T(8,128)(2,1)S(1)}, u32[]{:S(2)}, u32[]{:S(2)}) collective-permute-start(bf16[256,1024]{1,0:T(8,128)(2,1)S(1)} %collective-permute-done.22.refs_6_), channel_id=1, source_target_pairs={{0,1},{1,0},{2,3},{3,2},{4,5},{5,4},{6,7},{7,6},{8,9},{9,8},{10,11... | collective-permute-start | bytes 1572872 | tf_op jit(solution)/shard_map/ppermute | solution.py:24
  113.3 12.1 %collective-permute-start.43 = (bf16[256,512]{1,0:T(8,128)(2,1)S(1)}, bf16[256,512]{1,0:T(8,128)(2,1)S(1)}, u32[]{:S(2)}, u32[]{:S(2)}) collective-permute-start(bf16[256,512]{1,0:T(8,128)(2,1)S(1)} %constant_dynamic-update-slice_fusion.refs_15_), channel_id=1, source_target_pairs={{0,1},{1,0},{2,3},{3,2},{4,5},{5,4},{6,7},{7,6},{8,9},{9,8},{10,11... | collective-permute-start | bytes 786440 | tf_op jit(solution)/shard_map/ppermute | solution.py:24
  (17 other events, 130.6 us)

commit v4 on v3

--- a/solution.py
+++ b/solution.py
@@ -55,14 +55,6 @@
 
 def rows(value, start, count):
     return lax.dynamic_slice_in_dim(value, start, count, 0)
-
-
-def joined(mine, theirs, mine_second, axis):
-    return jnp.where(
-        mine_second == 1,
-        jnp.concatenate([theirs, mine], axis),
-        jnp.concatenate([mine, theirs], axis),
-    )
 
 
 def put(buffer, piece, start):
@@ -261,7 +253,9 @@
     one, two, three = [move(total, flip_x(bit)) for bit in (1, 2, 3)]
     total = (total + one) + (two + three)
     low = total.astype(BF)
-    low2 = joined(low, move(low, other_zh), zh, 1)
+    low2 = jnp.zeros((64, 512), BF)
+    low2 = lax.dynamic_update_slice_in_dim(low2, low, zh * 256, 1)
+    low2 = lax.dynamic_update_slice_in_dim(low2, move(low, other_zh), (1 - zh) * 256, 1)
     low3 = put(jnp.zeros((256, 512), BF), low2, y * 64)
     for step in (1, 2, 3):
         low3 = put(low3, move(low2, along_y(step)), ((y - step) % 4) * 64)

time: 139 us -> 138 us (level)
  waiting for transfers between devices: 52.8 us -> 56.2 us
  starting transfers between devices: 55.6 us -> 52.4 us
    ppermute x37, waiting for transfers between devices: 52.8 us -> 56.2 us  [move(): return lax.ppermute(value, ('row', 'col'), pairs)]
    ppermute x37, starting transfers between devices: 55.6 us -> 52.4 us  [move(): return lax.ppermute(value, ('row', 'col'), pairs)]
  transfers between devices with their start and end apart: 37 -> 37, of which waited for: 12 -> 13; matrix products, arithmetic and copies ran while one was open for 6% -> 6% of each run, Pallas kernels for 0% -> 0%
where the time goes in v4:
time: 138 us
  waiting for transfers between devices  56.2 us (41%)
  starting transfers between devices  52.4 us (38%)
  Pallas kernels  12 us (9%)
  matrix products  8.27 us (6%)
  other arithmetic  4.02 us (3%)
  between operations  2.34 us (2%)
  local copies, waits for them, and re-layouts  2.28 us (2%)
    ppermute x37, waiting for transfers between devices, move(): return lax.ppermute(value, ('row', 'col'), pairs)  56.2 us
    ppermute x37, starting transfers between devices, move(): return lax.ppermute(value, ('row', 'col'), pairs)  52.4 us
    pallas_call x1, Pallas kernels, tail(): pl.pallas_call(tail_kernel, grid_spec=pltpu.PrefetchScalarGridSpec(num_sc...  12 us
    dot_general x11, matrix products, mm(): return jnp.dot(a, b, preferred_element_type=F32)  8.01 us
  transfers between devices with their start and end apart: 37, of which 13 were waited for; matrix products, arithmetic and copies ran while one was open for 6% of the time, Pallas kernels for 0%

profile of v4, /device:TPU:8, one launch (start us, length us, event | category | flops | bytes accessed | tf_op | source)
XLA Modules:
  0.0 137.8 jit_solution(652792061183617482)
XLA Ops:
  9.2 2.4 %collective-permute-start.9 = (bf16[128,512]{1,0:T(8,128)(2,1)S(1)}, bf16[128,512]{1,0:T(8,128)(2,1)S(1)}, u32[]{:S(2)}, u32[]{:S(2)}) collective-permute-start(bf16[128,512]{1,0:T(8,128)(2,1)S(1)} %get-tuple-element.67), channel_id=1, source_target_pairs={{0,4},{1,5},{2,6},{3,7},{4,0},{5,1},{6,2},{7,3},{8,12},{9,13},{10,... | collective-permute-start | bytes 393224 | tf_op jit(solution)/shard_map/ppermute | solution.py:24
  11.6 4.7 %collective-permute-start.14 = (bf16[128,512]{1,0:T(8,128)(2,1)S(1)}, bf16[128,512]{1,0:T(8,128)(2,1)S(1)}, u32[]{:S(2)}, u32[]{:S(2)}) collective-permute-start(bf16[128,512]{1,0:T(8,128)(2,1)S(1)} %get-tuple-element.68), channel_id=1, source_target_pairs={{0,14},{1,15},{2,8},{3,9},{4,10},{5,11},{6,12},{7,13},{8,6},{9,7},... | collective-permute-start | bytes 393224 | tf_op jit(solution)/shard_map/ppermute | solution.py:24
  16.2 4.9 %collective-permute-start.12 = (bf16[128,512]{1,0:T(8,128)(2,1)S(1)}, bf16[128,512]{1,0:T(8,128)(2,1)S(1)}, u32[]{:S(2)}, u32[]{:S(2)}) collective-permute-start(bf16[128,512]{1,0:T(8,128)(2,1)S(1)} %get-tuple-element.70), channel_id=1, source_target_pairs={{0,10},{1,11},{2,12},{3,13},{4,14},{5,15},{6,8},{7,9},{8,2},{9,3},... | collective-permute-start | bytes 393224 | tf_op jit(solution)/shard_map/ppermute | solution.py:24
  23.3 5.0 %collective-permute-done.8 = bf16[128,512]{1,0:T(8,128)(2,1)S(1)} collective-permute-done((bf16[128,512]{1,0:T(8,128)(2,1)S(1)}, bf16[128,512]{1,0:T(8,128)(2,1)S(1)}, u32[]{:S(2)}, u32[]{:S(2)}) %collective-permute-start.8) | collective-permute-done | bytes 131104 | tf_op jit(solution)/shard_map/ppermute | solution.py:24
  28.3 2.0 %collective-permute-start.10 = (bf16[128,512]{1,0:T(8,128)(2,1)S(1)}, bf16[128,512]{1,0:T(8,128)(2,1)S(1)}, u32[]{:S(2)}, u32[]{:S(2)}) collective-permute-start(bf16[128,512]{1,0:T(8,128)(2,1)S(1)} %get-tuple-element.72), channel_id=1, source_target_pairs={{0,6},{1,7},{2,0},{3,1},{4,2},{5,3},{6,4},{7,5},{8,14},{9,15},{10,... | collective-permute-start | bytes 393224 | tf_op jit(solution)/shard_map/ppermute | solution.py:24
  30.9 2.4 %collective-permute-done.10 = bf16[128,512]{1,0:T(8,128)(2,1)S(1)} collective-permute-done((bf16[128,512]{1,0:T(8,128)(2,1)S(1)}, bf16[128,512]{1,0:T(8,128)(2,1)S(1)}, u32[]{:S(2)}, u32[]{:S(2)}) %collective-permute-start.10) | collective-permute-done | bytes 131104 | tf_op jit(solution)/shard_map/ppermute | solution.py:24
  33.3 3.2 %collective-permute-start.11 = (bf16[128,512]{1,0:T(8,128)(2,1)S(1)}, bf16[128,512]{1,0:T(8,128)(2,1)S(1)}, u32[]{:S(2)}, u32[]{:S(2)}) collective-permute-start(bf16[128,512]{1,0:T(8,128)(2,1)S(1)} %get-tuple-element.71), channel_id=1, source_target_pairs={{0,8},{1,9},{2,10},{3,11},{4,12},{5,13},{6,14},{7,15},{8,0},{9,1},... | collective-permute-start | bytes 393224 | tf_op jit(solution)/shard_map/ppermute | solution.py:24
  37.0 2.8 %collective-permute-done.11 = bf16[128,512]{1,0:T(8,128)(2,1)S(1)} collective-permute-done((bf16[128,512]{1,0:T(8,128)(2,1)S(1)}, bf16[128,512]{1,0:T(8,128)(2,1)S(1)}, u32[]{:S(2)}, u32[]{:S(2)}) %collective-permute-start.11) | collective-permute-done | bytes 131104 | tf_op jit(solution)/shard_map/ppermute | solution.py:24
  44.7 3.2 %collective-permute-start.21 = (bf16[128,1024]{1,0:T(8,128)(2,1)S(1)}, bf16[128,1024]{1,0:T(8,128)(2,1)S(1)}, u32[]{:S(2)}, u32[]{:S(2)}) collective-permute-start(bf16[128,1024]{1,0:T(8,128)(2,1)S(1)} %fusion.46), channel_id=1, source_target_pairs={{0,8},{1,9},{2,10},{3,11},{4,12},{5,13},{6,14},{7,15},{8,0},{9,1},... | collective-permute-start | bytes 786440 | tf_op jit(solution)/shard_map/ppermute | solution.py:24
  48.0 4.6 %collective-permute-done.21 = bf16[128,1024]{1,0:T(8,128)(2,1)S(1)} collective-permute-done((bf16[128,1024]{1,0:T(8,128)(2,1)S(1)}, bf16[128,1024]{1,0:T(8,128)(2,1)S(1)}, u32[]{:S(2)}, u32[]{:S(2)}) %collective-permute-start.21) | collective-permute-done | bytes 262176 | tf_op jit(solution)/shard_map/ppermute | solution.py:24
  53.1 3.8 %collective-permute-start.24 = (bf16[128,1024]{1,0:T(8,128)(2,1)S(1)}, bf16[128,1024]{1,0:T(8,128)(2,1)S(1)}, u32[]{:S(2)}, u32[]{:S(2)}) collective-permute-start(bf16[128,1024]{1,0:T(8,128)(2,1)S(1)} %fusion.46), channel_id=1, source_target_pairs={{0,4},{1,5},{2,6},{3,7},{4,0},{5,1},{6,2},{7,3},{8,12},{9,13},{10,... | collective-permute-start | bytes 786440 | tf_op jit(solution)/shard_map/ppermute | solution.py:24
  60.5 3.6 %collective-permute-start.15 = (bf16[128,1024]{1,0:T(8,128)(2,1)S(1)}, bf16[128,1024]{1,0:T(8,128)(2,1)S(1)}, u32[]{:S(2)}, u32[]{:S(2)}) collective-permute-start(bf16[128,1024]{1,0:T(8,128)(2,1)S(1)} %fusion.46), channel_id=1, source_target_pairs={{0,0},{1,1},{2,32},{3,33},{4,64},{5,65},{6,96},{7,97},{8,16},{9,17... | collective-permute-start | bytes 786440 | tf_op jit(solution)/shard_map/ppermute | solution.py:24
  64.9 2.2 %collective-permute-start.25 = (bf16[128,1024]{1,0:T(8,128)(2,1)S(1)}, bf16[128,1024]{1,0:T(8,128)(2,1)S(1)}, u32[]{:S(2)}, u32[]{:S(2)}) collective-permute-start(bf16[128,1024]{1,0:T(8,128)(2,1)S(1)} %collective-permute-done.24.refs_8_), channel_id=1, source_target_pairs={{0,8},{1,9},{2,10},{3,11},{4,12},{5,13},{6,14},{7,15},{8,0},{9,1},... | collective-permute-start | bytes 786440 | tf_op jit(solution)/shard_map/ppermute | solution.py:24
  67.1 5.2 %collective-permute-done.33 = f32[64,256]{1,0:T(8,128)S(1)} collective-permute-done((f32[64,256]{1,0:T(8,128)S(1)}, f32[64,256]{1,0:T(8,128)S(1)}, u32[]{:S(2)}, u32[]{:S(2)}) %collective-permute-start.33) | collective-permute-done | bytes 65568 | tf_op jit(solution)/shard_map/ppermute | solution.py:24
  72.5 7.1 %collective-permute-done.15 = bf16[128,1024]{1,0:T(8,128)(2,1)S(1)} collective-permute-done((bf16[128,1024]{1,0:T(8,128)(2,1)S(1)}, bf16[128,1024]{1,0:T(8,128)(2,1)S(1)}, u32[]{:S(2)}, u32[]{:S(2)}) %collective-permute-start.15) | collective-permute-done | bytes 262176 | tf_op jit(solution)/shard_map/ppermute | solution.py:24
  82.0 2.9 %collective-permute-start.37 = (f32[64,256]{1,0:T(8,128)S(1)}, f32[64,256]{1,0:T(8,128)S(1)}, u32[]{:S(2)}, u32[]{:S(2)}) collective-permute-start(f32[64,256]{1,0:T(8,128)S(1)} %add.537), channel_id=1, source_target_pairs={{0,64},{1,65},{2,66},{3,67},{4,68},{5,69},{6,70},{7,71},{8,72},{9,... | collective-permute-start | bytes 196616 | tf_op jit(solution)/shard_map/ppermute | solution.py:24
  85.0 5.5 %collective-permute-done.38 = f32[64,256]{1,0:T(8,128)S(1)} collective-permute-done((f32[64,256]{1,0:T(8,128)S(1)}, f32[64,256]{1,0:T(8,128)S(1)}, u32[]{:S(2)}, u32[]{:S(2)}) %collective-permute-start.38) | collective-permute-done | bytes 65568 | tf_op jit(solution)/shard_map/ppermute | solution.py:24
  90.5 2.0 %collective-permute-start.22 = (bf16[256,1024]{1,0:T(8,128)(2,1)S(1)}, bf16[256,1024]{1,0:T(8,128)(2,1)S(1)}, u32[]{:S(2)}, u32[]{:S(2)}) collective-permute-start(bf16[256,1024]{1,0:T(8,128)(2,1)S(1)} %constant_dynamic-update-slice_fusion.6.refs_5_), channel_id=1, source_target_pairs={{0,2},{1,3},{2,4},{3,5},{4,6},{5,7},{6,0},{7,1},{8,10},{9,11},{10,... | collective-permute-start | bytes 1572872 | tf_op jit(solution)/shard_map/ppermute | solution.py:24
  94.0 7.3 %collective-permute-done.39 = bf16[64,256]{1,0:T(8,128)(2,1)S(1)} collective-permute-done((bf16[64,256]{1,0:T(8,128)(2,1)S(1)}, bf16[64,256]{1,0:T(8,128)(2,1)S(1)}, u32[]{:S(2)}, u32[]{:S(2)}) %collective-permute-start.39) | collective-permute-done | bytes 32800 | tf_op jit(solution)/shard_map/ppermute | solution.py:24
  103.6 2.6 %collective-permute-done.40 = bf16[64,512]{1,0:T(8,128)(2,1)S(1)} collective-permute-done((bf16[64,512]{1,0:T(8,128)(2,1)S(1)}, bf16[64,512]{1,0:T(8,128)(2,1)S(1)}, u32[]{:S(2)}, u32[]{:S(2)}) %collective-permute-start.40) | collective-permute-done | bytes 65568 | tf_op jit(solution)/shard_map/ppermute | solution.py:24
  107.8 3.6 %collective-permute-start.18 = (bf16[256,1024]{1,0:T(8,128)(2,1)S(1)}, bf16[256,1024]{1,0:T(8,128)(2,1)S(1)}, u32[]{:S(2)}, u32[]{:S(2)}) collective-permute-start(bf16[256,1024]{1,0:T(8,128)(2,1)S(1)} %constant_dynamic-update-slice_fusion.8.refs_0_), channel_id=1, source_target_pairs={{0,96},{1,97},{2,98},{3,99},{4,100},{5,101},{6,102},{7,103},{8,104... | collective-permute-start | bytes 1572872 | tf_op jit(solution)/shard_map/ppermute | solution.py:24
  113.0 9.1 %collective-permute-done.18.refs_2_ = bf16[256,1024]{1,0:T(8,128)(2,1)S(1)} collective-permute-done((bf16[256,1024]{1,0:T(8,128)(2,1)S(1)}, bf16[256,1024]{1,0:T(8,128)(2,1)S(1)}, u32[]{:S(2)}, u32[]{:S(2)}) %collective-permute-start.18) | collective-permute-done | bytes 524320 | tf_op jit(solution)/shard_map/ppermute | solution.py:24
  122.1 3.4 %collective-permute-done.17.refs_1_ = bf16[256,1024]{1,0:T(8,128)(2,1)S(1)} collective-permute-done((bf16[256,1024]{1,0:T(8,128)(2,1)S(1)}, bf16[256,1024]{1,0:T(8,128)(2,1)S(1)}, u32[]{:S(2)}, u32[]{:S(2)}) %collective-permute-start.17) | collective-permute-done | bytes 524320 | tf_op jit(solution)/shard_map/ppermute | solution.py:24
  125.6 12.0 %shard_map.86 = (f32[2048,1024]{1,0:T(8,128)}, bf16[2048,1024]{1,0:T(8,128)(2,1)}) custom-call(s32[17]{0:T(128)S(1)} %pad_add_fusion.spot, bf16[256,1024]{1,0:T(8,128)(2,1)S(1)} %constant_dynamic-update-slice_fusion.8.refs_0_, bf16[256,1024]{1,0:T(8,128)(2,1)S(1)} %collective-permute-done.17.refs_1_, bf16[256,1024]{1,0:T(8,128)(2,1)S(1)} %collective-permute-done.18.refs_2_, ...), custom_call_target="tpu_custom_call" | custom-call | flops 8999999488 | bytes 29360128 | tf_op jit(solution)/shard_map/pallas_call | solution.py:151
  (108 shorter events, 29.9 us)
Async XLA Ops:
  9.2 32.8 %collective-permute-start.9 = (bf16[128,512]{1,0:T(8,128)(2,1)S(1)}, bf16[128,512]{1,0:T(8,128)(2,1)S(1)}, u32[]{:S(2)}, u32[]{:S(2)}) collective-permute-start(bf16[128,512]{1,0:T(8,128)(2,1)S(1)} %get-tuple-element.67), channel_id=1, source_target_pairs={{0,4},{1,5},{2,6},{3,7},{4,0},{5,1},{6,2},{7,3},{8,12},{9,13},{10,... | collective-permute-start | bytes 393224 | tf_op jit(solution)/shard_map/ppermute | solution.py:24
  11.6 29.9 %collective-permute-start.14 = (bf16[128,512]{1,0:T(8,128)(2,1)S(1)}, bf16[128,512]{1,0:T(8,128)(2,1)S(1)}, u32[]{:S(2)}, u32[]{:S(2)}) collective-permute-start(bf16[128,512]{1,0:T(8,128)(2,1)S(1)} %get-tuple-element.68), channel_id=1, source_target_pairs={{0,14},{1,15},{2,8},{3,9},{4,10},{5,11},{6,12},{7,13},{8,6},{9,7},... | collective-permute-start | bytes 393224 | tf_op jit(solution)/shard_map/ppermute | solution.py:24
  16.2 24.6 %collective-permute-start.13 = (bf16[128,512]{1,0:T(8,128)(2,1)S(1)}, bf16[128,512]{1,0:T(8,128)(2,1)S(1)}, u32[]{:S(2)}, u32[]{:S(2)}) collective-permute-start(bf16[128,512]{1,0:T(8,128)(2,1)S(1)} %get-tuple-element.69), channel_id=1, source_target_pairs={{0,12},{1,13},{2,14},{3,15},{4,8},{5,9},{6,10},{7,11},{8,4},{9,5},... | collective-permute-start | bytes 393224 | tf_op jit(solution)/shard_map/ppermute | solution.py:24
  16.2 24.1 %collective-permute-start.12 = (bf16[128,512]{1,0:T(8,128)(2,1)S(1)}, bf16[128,512]{1,0:T(8,128)(2,1)S(1)}, u32[]{:S(2)}, u32[]{:S(2)}) collective-permute-start(bf16[128,512]{1,0:T(8,128)(2,1)S(1)} %get-tuple-element.70), channel_id=1, source_target_pairs={{0,10},{1,11},{2,12},{3,13},{4,14},{5,15},{6,8},{7,9},{8,2},{9,3},... | collective-permute-start | bytes 393224 | tf_op jit(solution)/shard_map/ppermute | solution.py:24
  53.1 11.0 %collective-permute-start.24 = (bf16[128,1024]{1,0:T(8,128)(2,1)S(1)}, bf16[128,1024]{1,0:T(8,128)(2,1)S(1)}, u32[]{:S(2)}, u32[]{:S(2)}) collective-permute-start(bf16[128,1024]{1,0:T(8,128)(2,1)S(1)} %fusion.46), channel_id=1, source_target_pairs={{0,4},{1,5},{2,6},{3,7},{4,0},{5,1},{6,2},{7,3},{8,12},{9,13},{10,... | collective-permute-start | bytes 786440 | tf_op jit(solution)/shard_map/ppermute | solution.py:24
  57.1 10.0 %collective-permute-start.34 = (f32[64,256]{1,0:T(8,128)S(1)}, f32[64,256]{1,0:T(8,128)S(1)}, u32[]{:S(2)}, u32[]{:S(2)}) collective-permute-start(f32[64,256]{1,0:T(8,128)S(1)} %get-tuple-element.75), channel_id=1, source_target_pairs={{0,6},{1,7},{2,0},{3,1},{4,2},{5,3},{6,4},{7,5},{8,14},{9,15},{10,... | collective-permute-start | bytes 196616 | tf_op jit(solution)/shard_map/ppermute | solution.py:24
  59.1 13.2 %collective-permute-start.33 = (f32[64,256]{1,0:T(8,128)S(1)}, f32[64,256]{1,0:T(8,128)S(1)}, u32[]{:S(2)}, u32[]{:S(2)}) collective-permute-start(f32[64,256]{1,0:T(8,128)S(1)} %get-tuple-element.76), channel_id=1, source_target_pairs={{0,4},{1,5},{2,6},{3,7},{4,0},{5,1},{6,2},{7,3},{8,12},{9,13},{10,... | collective-permute-start | bytes 196616 | tf_op jit(solution)/shard_map/ppermute | solution.py:24
  60.5 19.0 %collective-permute-start.15 = (bf16[128,1024]{1,0:T(8,128)(2,1)S(1)}, bf16[128,1024]{1,0:T(8,128)(2,1)S(1)}, u32[]{:S(2)}, u32[]{:S(2)}) collective-permute-start(bf16[128,1024]{1,0:T(8,128)(2,1)S(1)} %fusion.46), channel_id=1, source_target_pairs={{0,0},{1,1},{2,32},{3,33},{4,64},{5,65},{6,96},{7,97},{8,16},{9,17... | collective-permute-start | bytes 786440 | tf_op jit(solution)/shard_map/ppermute | solution.py:24
  64.1 17.9 %collective-permute-start.29 = (bf16[128,1024]{1,0:T(8,128)(2,1)S(1)}, bf16[128,1024]{1,0:T(8,128)(2,1)S(1)}, u32[]{:S(2)}, u32[]{:S(2)}) collective-permute-start(bf16[128,1024]{1,0:T(8,128)(2,1)S(1)} %collective-permute-done.24.refs_8_), channel_id=1, source_target_pairs={{0,1},{1,0},{2,3},{3,2},{4,5},{5,4},{6,7},{7,6},{8,9},{9,8},{10,11... | collective-permute-start | bytes 786440 | tf_op jit(solution)/shard_map/ppermute | solution.py:24
  64.9 20.0 %collective-permute-start.25 = (bf16[128,1024]{1,0:T(8,128)(2,1)S(1)}, bf16[128,1024]{1,0:T(8,128)(2,1)S(1)}, u32[]{:S(2)}, u32[]{:S(2)}) collective-permute-start(bf16[128,1024]{1,0:T(8,128)(2,1)S(1)} %collective-permute-done.24.refs_8_), channel_id=1, source_target_pairs={{0,8},{1,9},{2,10},{3,11},{4,12},{5,13},{6,14},{7,15},{8,0},{9,1},... | collective-permute-start | bytes 786440 | tf_op jit(solution)/shard_map/ppermute | solution.py:24
  79.5 13.1 %collective-permute-start.19 = (bf16[128,1024]{1,0:T(8,128)(2,1)S(1)}, bf16[128,1024]{1,0:T(8,128)(2,1)S(1)}, u32[]{:S(2)}, u32[]{:S(2)}) collective-permute-start(bf16[128,1024]{1,0:T(8,128)(2,1)S(1)} %collective-permute-done.15), channel_id=1, source_target_pairs={{0,64},{1,65},{2,66},{3,67},{4,68},{5,69},{6,70},{7,71},{8,72},{9,... | collective-permute-start | bytes 786440 | tf_op jit(solution)/shard_map/ppermute | solution.py:24
  80.5 12.2 %collective-permute-start.16 = (bf16[128,1024]{1,0:T(8,128)(2,1)S(1)}, bf16[128,1024]{1,0:T(8,128)(2,1)S(1)}, u32[]{:S(2)}, u32[]{:S(2)}) collective-permute-start(bf16[128,1024]{1,0:T(8,128)(2,1)S(1)} %collective-permute-done.15), channel_id=1, source_target_pairs={{0,16},{1,17},{2,18},{3,19},{4,20},{5,21},{6,22},{7,23},{8,24},{9,... | collective-permute-start | bytes 786440 | tf_op jit(solution)/shard_map/ppermute | solution.py:24
  80.5 10.0 %collective-permute-start.38 = (f32[64,256]{1,0:T(8,128)S(1)}, f32[64,256]{1,0:T(8,128)S(1)}, u32[]{:S(2)}, u32[]{:S(2)}) collective-permute-start(f32[64,256]{1,0:T(8,128)S(1)} %add.537), channel_id=1, source_target_pairs={{0,96},{1,97},{2,98},{3,99},{4,100},{5,101},{6,102},{7,103},{8,104... | collective-permute-start | bytes 196616 | tf_op jit(solution)/shard_map/ppermute | solution.py:24
  90.5 17.3 %collective-permute-start.23 = (bf16[256,1024]{1,0:T(8,128)(2,1)S(1)}, bf16[256,1024]{1,0:T(8,128)(2,1)S(1)}, u32[]{:S(2)}, u32[]{:S(2)}) collective-permute-start(bf16[256,1024]{1,0:T(8,128)(2,1)S(1)} %constant_dynamic-update-slice_fusion.6.refs_5_), channel_id=1, source_target_pairs={{0,6},{1,7},{2,0},{3,1},{4,2},{5,3},{6,4},{7,5},{8,14},{9,15},{10,... | collective-permute-start | bytes 1572872 | tf_op jit(solution)/shard_map/ppermute | solution.py:24
  90.5 20.9 %collective-permute-start.22 = (bf16[256,1024]{1,0:T(8,128)(2,1)S(1)}, bf16[256,1024]{1,0:T(8,128)(2,1)S(1)}, u32[]{:S(2)}, u32[]{:S(2)}) collective-permute-start(bf16[256,1024]{1,0:T(8,128)(2,1)S(1)} %constant_dynamic-update-slice_fusion.6.refs_5_), channel_id=1, source_target_pairs={{0,2},{1,3},{2,4},{3,5},{4,6},{5,7},{6,0},{7,1},{8,10},{9,11},{10,... | collective-permute-start | bytes 1572872 | tf_op jit(solution)/shard_map/ppermute | solution.py:24
  92.5 8.8 %collective-permute-start.30 = (bf16[128,1024]{1,0:T(8,128)(2,1)S(1)}, bf16[128,1024]{1,0:T(8,128)(2,1)S(1)}, u32[]{:S(2)}, u32[]{:S(2)}) collective-permute-start(bf16[128,1024]{1,0:T(8,128)(2,1)S(1)} %collective-permute-done.25.refs_9_), channel_id=1, source_target_pairs={{0,1},{1,0},{2,3},{3,2},{4,5},{5,4},{6,7},{7,6},{8,9},{9,8},{10,11... | collective-permute-start | bytes 786440 | tf_op jit(solution)/shard_map/ppermute | solution.py:24
  92.6 10.3 %collective-permute-start.20 = (bf16[128,1024]{1,0:T(8,128)(2,1)S(1)}, bf16[128,1024]{1,0:T(8,128)(2,1)S(1)}, u32[]{:S(2)}, u32[]{:S(2)}) collective-permute-start(bf16[128,1024]{1,0:T(8,128)(2,1)S(1)} %collective-permute-done.19.refs_3_), channel_id=1, source_target_pairs={{0,16},{1,17},{2,18},{3,19},{4,20},{5,21},{6,22},{7,23},{8,24},{9,... | collective-permute-start | bytes 786440 | tf_op jit(solution)/shard_map/ppermute | solution.py:24
  92.7 8.6 %collective-permute-start.39 = (bf16[64,256]{1,0:T(8,128)(2,1)S(1)}, bf16[64,256]{1,0:T(8,128)(2,1)S(1)}, u32[]{:S(2)}, u32[]{:S(2)}) collective-permute-start(bf16[64,256]{1,0:T(8,128)(2,1)S(1)} %get-tuple-element.43), channel_id=1, source_target_pairs={{0,8},{1,9},{2,10},{3,11},{4,12},{5,13},{6,14},{7,15},{8,0},{9,1},... | collective-permute-start | bytes 98312 | tf_op jit(solution)/shard_map/ppermute | solution.py:24
  101.3 10.8 %collective-permute-start.26 = (bf16[256,1024]{1,0:T(8,128)(2,1)S(1)}, bf16[256,1024]{1,0:T(8,128)(2,1)S(1)}, u32[]{:S(2)}, u32[]{:S(2)}) collective-permute-start(bf16[256,1024]{1,0:T(8,128)(2,1)S(1)} %constant_dynamic-update-slice_fusion.6.refs_5_), channel_id=1, source_target_pairs={{0,1},{1,0},{2,3},{3,2},{4,5},{5,4},{6,7},{7,6},{8,9},{9,8},{10,11... | collective-permute-start | bytes 1572872 | tf_op jit(solution)/shard_map/ppermute | solution.py:24
  107.8 14.3 %collective-permute-start.18 = (bf16[256,1024]{1,0:T(8,128)(2,1)S(1)}, bf16[256,1024]{1,0:T(8,128)(2,1)S(1)}, u32[]{:S(2)}, u32[]{:S(2)}) collective-permute-start(bf16[256,1024]{1,0:T(8,128)(2,1)S(1)} %constant_dynamic-update-slice_fusion.8.refs_0_), channel_id=1, source_target_pairs={{0,96},{1,97},{2,98},{3,99},{4,100},{5,101},{6,102},{7,103},{8,104... | collective-permute-start | bytes 1572872 | tf_op jit(solution)/shard_map/ppermute | solution.py:24
  111.4 14.1 %collective-permute-start.17 = (bf16[256,1024]{1,0:T(8,128)(2,1)S(1)}, bf16[256,1024]{1,0:T(8,128)(2,1)S(1)}, u32[]{:S(2)}, u32[]{:S(2)}) collective-permute-start(bf16[256,1024]{1,0:T(8,128)(2,1)S(1)} %constant_dynamic-update-slice_fusion.8.refs_0_), channel_id=1, source_target_pairs={{0,32},{1,33},{2,34},{3,35},{4,36},{5,37},{6,38},{7,39},{8,40},{9,... | collective-permute-start | bytes 1572872 | tf_op jit(solution)/shard_map/ppermute | solution.py:24
  111.5 14.1 %collective-permute-start.28 = (bf16[256,1024]{1,0:T(8,128)(2,1)S(1)}, bf16[256,1024]{1,0:T(8,128)(2,1)S(1)}, u32[]{:S(2)}, u32[]{:S(2)}) collective-permute-start(bf16[256,1024]{1,0:T(8,128)(2,1)S(1)} %collective-permute-done.23.refs_7_), channel_id=1, source_target_pairs={{0,1},{1,0},{2,3},{3,2},{4,5},{5,4},{6,7},{7,6},{8,9},{9,8},{10,11... | collective-permute-start | bytes 1572872 | tf_op jit(solution)/shard_map/ppermute | solution.py:24
  111.9 13.6 %collective-permute-start.27 = (bf16[256,1024]{1,0:T(8,128)(2,1)S(1)}, bf16[256,1024]{1,0:T(8,128)(2,1)S(1)}, u32[]{:S(2)}, u32[]{:S(2)}) collective-permute-start(bf16[256,1024]{1,0:T(8,128)(2,1)S(1)} %collective-permute-done.22.refs_6_), channel_id=1, source_target_pairs={{0,1},{1,0},{2,3},{3,2},{4,5},{5,4},{6,7},{7,6},{8,9},{9,8},{10,11... | collective-permute-start | bytes 1572872 | tf_op jit(solution)/shard_map/ppermute | solution.py:24
  112.1 13.5 %collective-permute-start.43 = (bf16[256,512]{1,0:T(8,128)(2,1)S(1)}, bf16[256,512]{1,0:T(8,128)(2,1)S(1)}, u32[]{:S(2)}, u32[]{:S(2)}) collective-permute-start(bf16[256,512]{1,0:T(8,128)(2,1)S(1)} %constant_dynamic-update-slice_fusion.refs_15_), channel_id=1, source_target_pairs={{0,1},{1,0},{2,3},{3,2},{4,5},{5,4},{6,7},{7,6},{8,9},{9,8},{10,11... | collective-permute-start | bytes 786440 | tf_op jit(solution)/shard_map/ppermute | solution.py:24
  (17 other events, 117.3 us)
